TPU v7x, 32 devices: a whole 2x2x4 slice. The times are simulated.
32 devices in a mesh: rep: 8 (over y, x, core), shard: 4 (over z).
Axes of the slice: x: 2, y: 2, z: 4, core: 2. Of those that a mesh axis runs over, the one named last changes fastest.
Arguments:
- tokens: bfloat16 [8192, 512], P(('rep', 'shard')), may hold values from -6 to 6
- cotangent: bfloat16 [8192, 512], P(('rep', 'shard')), may hold values from -6 to 6
- block_fill: int32 [64], P(('rep', 'shard')), may hold values from 0 to 128, as said below
- block_start: int32 [64], P(('rep', 'shard')), may hold values from 0 to 1, as said below
- in_weight: float32 [512, 2320], P('shard'), may hold values from -0.25 to 0.25
- out_weight: float32 [1024, 512], P('shard'), may hold values from -0.1875 to 0.1875
- in_moment: float32 [512, 2320], P('shard'), may hold values from -1.5 to 1.5
- out_moment: float32 [1024, 512], P('shard'), may hold values from -4 to 4
- norm_gain: float32 [512], replicated, may hold values from 0.5 to 1.5
- gate_gain: float32 [1024], replicated, may hold values from 0.5 to 1.5
- conv_params: float32 [5, 1280], replicated, may hold values from -0.5 to 0.5
- head_params: float32 [3, 16], replicated, may hold values from -6.3 to 1.5
- adam_norm: float32 [2, 512], replicated, may hold values from -0.2 to 0.2, as said below
- adam_gate: float32 [2, 1024], replicated, may hold values from -0.2 to 0.2, as said below
- adam_conv: float32 [2, 5, 1280], replicated, may hold values from -0.2 to 0.2, as said below
- adam_head: float32 [2, 3, 16], replicated, may hold values from -0.2 to 0.2, as said below
Outputs:
- activations: bfloat16 [8192, 512], P(('rep', 'shard'))
- input_grad: float32 [8192, 512], P(('rep', 'shard'))
- grad_in_weight: float32 [512, 2320], P('shard')
- grad_out_weight: float32 [1024, 512], P('shard')
- grad_norm_gain: float32 [512], replicated
- grad_gate_gain: float32 [1024], replicated
- grad_conv: float32 [5, 1280], replicated
- grad_head: float32 [3, 16], replicated
- new_in_weight: float32 [512, 2320], P('shard')
- new_out_weight: float32 [1024, 512], P('shard')
- new_in_moment: float32 [512, 2320], P('shard')
- new_out_moment: float32 [1024, 512], P('shard')
- new_norm_gain: float32 [512], replicated
- new_gate_gain: float32 [1024], replicated
- new_conv_params: float32 [5, 1280], replicated
- new_head_params: float32 [3, 16], replicated
- new_adam_norm: float32 [2, 512], replicated
- new_adam_gate: float32 [2, 1024], replicated
- new_adam_conv: float32 [2, 5, 1280], replicated
- new_adam_head: float32 [2, 3, 16], replicated
Inputs may be any that keep to these rules, and one draw needn't show every extreme that they name: Each device holds 2 blocks of 128 slots, in order; a block's first block_fill slots hold tokens of one sequence and the rest are padding. A sequence fills every block but its last. Some device holds a sequence of 256 tokens, and some device has an empty block. `block_start`: 1 on every device's first block, on every block that follows a partly filled or empty one, and on empty blocks; 0 only where the block before is full and the sequence goes on. `adam_norm`: second moments are positive. `adam_gate`: second moments are positive. `adam_conv`: second moments are positive. `adam_head`: second moments are positive.
All inputs are finite; a program needn't handle non-finite values.
Results may differ from a plain program's by a relative error of at most 0.0085.
The roundings to bfloat16 on the way count: a program that leaves them out, or rounds other values in their place, can miss the bound.
Values may be sent and summed in bfloat16 or wider, within the bound.
A program may use at most 128 MiB of HBM per device.

v0:
```python
import math

import jax
import jax.numpy as jnp
from jax import lax
from jax.experimental import pallas as pl
from jax.experimental.pallas import tpu as pltpu
from jax.sharding import PartitionSpec as P

NS_STEPS = 5
ADAM_STEP = 3


ssd_precision = lax.Precision.HIGH
norm_eps = 1e-05
schulz_coeffs = (3.4445, -4.775, 2.0315)
momentum_keep = 0.95
muon_rate = 0.05
adam_rate = 0.2
beta_first = 0.9
beta_second = 0.95
decay_rate = 0.1
adam_eps = 1e-08


def pre_norm(base, gain):
    return base * lax.rsqrt(jnp.mean(base * base, -1, keepdims=True) + norm_eps) * gain


def mixer(proj, conv_params, head_params, gate_gain, starts):
    total = proj.shape[0]
    blocks = starts.shape[0]
    length = total // blocks
    width_inner = gate_gain.shape[0]
    heads = head_params.shape[1]
    head_size = width_inner // heads
    taps = conv_params.shape[0] - 1
    channels = conv_params.shape[1]
    state_size = (channels - width_inner) // 2
    gate_in = proj[:, :width_inner]
    conv_in = proj[:, width_inner : width_inner + channels]
    dt_raw = proj[:, width_inner + channels :]
    seq_block = jnp.cumsum(starts)
    seq_token = jnp.repeat(seq_block, length)
    summed = conv_params[taps] + conv_params[taps - 1] * conv_in
    for offset in range(1, taps):
        moved = jnp.concatenate([jnp.zeros((offset, channels), jnp.float32), conv_in[:-offset]], 0)
        moved_seq = jnp.concatenate([jnp.full((offset,), -1, jnp.int32), seq_token[:-offset]], 0)
        same_seq = (moved_seq == seq_token).astype(jnp.float32)
        summed = summed + conv_params[taps - 1 - offset] * moved * same_seq[:, None]
    activated = jax.nn.silu(summed)
    values = activated[:, :width_inner].reshape(total, heads, head_size)
    b_input = activated[:, width_inner : width_inner + state_size]
    c_input = activated[:, width_inner + state_size :]
    step_size = jax.nn.softplus(dt_raw + head_params[0])
    rates = -jnp.exp(head_params[1])
    lower = jnp.tril(jnp.ones((total, total), jnp.bool_))
    mask = jnp.logical_and(lower, seq_token[:, None] == seq_token[None, :])
    columns = jnp.einsum(
        "ts,sh->ht", lower.astype(jnp.float32), step_size * rates, precision=lax.Precision.HIGHEST
    )
    spread = columns[:, :, None] - columns[:, None, :]
    decay = jnp.where(mask, jnp.exp(jnp.where(mask, spread, 0.0)), 0.0)
    scores = jnp.dot(c_input, b_input.T, precision=ssd_precision)
    weighted = values * step_size[:, :, None]
    outputs = jnp.einsum(
        "hts,shp->thp", decay * scores[None], weighted, precision=ssd_precision
    )
    outputs = outputs + head_params[2][None, :, None] * values
    gated = outputs.reshape(total, width_inner) * jax.nn.silu(gate_in)
    return gated * lax.rsqrt(jnp.mean(gated * gated, -1, keepdims=True) + norm_eps) * gate_gain


def device_pass(
    tokens,
    cotangent,
    fill,
    starts,
    fwd_in,
    fwd_out,
    back_in,
    back_out,
    norm_gain,
    gate_gain,
    conv_params,
    head_params,
):
    total = tokens.shape[0]
    length = total // fill.shape[0]
    position = jnp.arange(total, dtype=jnp.int32) % length
    live = position < jnp.repeat(fill, length)
    base = tokens.astype(jnp.float32)
    normed, norm_back = jax.vjp(pre_norm, base, norm_gain)
    normed16 = normed.astype(jnp.bfloat16)
    proj = jnp.dot(normed16, fwd_in, preferred_element_type=jnp.float32)

    def mix_piece(proj_in, conv_in, head_in, gain_in):
        return mixer(proj_in, conv_in, head_in, gain_in, starts)

    mixed, mixer_back = jax.vjp(mix_piece, proj, conv_params, head_params, gate_gain)
    mixed16 = mixed.astype(jnp.bfloat16)
    branch = jnp.dot(mixed16, fwd_out, preferred_element_type=jnp.float32)
    activations = jnp.where(live[:, None], base + branch, 0.0).astype(jnp.bfloat16)
    live_cot = jnp.where(live[:, None], cotangent, jnp.zeros_like(cotangent))
    d_mixed = jnp.dot(live_cot, back_out.T, preferred_element_type=jnp.float32)
    grad_out = jnp.dot(mixed16.T, live_cot, preferred_element_type=jnp.float32)
    d_proj, grad_conv, grad_head, grad_gate = mixer_back(d_mixed)
    d_proj16 = d_proj.astype(jnp.bfloat16)
    grad_in = jnp.dot(normed16.T, d_proj16, preferred_element_type=jnp.float32)
    d_normed = jnp.dot(d_proj16, back_in.T, preferred_element_type=jnp.float32)
    d_base, grad_norm = norm_back(d_normed)
    input_grad = live_cot.astype(jnp.float32) + d_base
    return (activations, input_grad, grad_in, grad_out, grad_norm, grad_gate, grad_conv, grad_head)


def muon_kernel(
    mats, ret, buf, cur, gram_ref, poly_ref,
    zs, zr, cs, cr, ps, pr, zs2, zr2, cs2, cr2, ps2, pr2,
):
    rep, shard, core, chip, chips, shards = places()
    partner = {"rep": 2 * chip + 1 - core}
    count = mats.shape[0]
    rows, wide = mats.shape[3:]
    tall = shards * chips * 2 * rows
    f32 = jnp.float32
    half = jnp.bfloat16
    owners = [number * shards // count for number in range(count)]
    others = [lax.rem(shard + step, shards) for step in range(1, shards)]
    moves = [lax.rem(chip + move, chips) for move in range(1, chips)]
    greet_peers(core, chip, shard, chips, shards)

    def to_owner(number, slot):
        return remote(
            mats.at[number, chip, core], buf.at[slot, chip, core],
            zs.at[number], zr.at[slot], {"shard": owners[number]},
        )

    for number in range(count):

        @pl.when(shard != owners[number])
        def _():
            to_owner(number, shard).start()

        @pl.when(shard == owners[number])
        def _():
            buf[shard] = mats[number]

    def own_work():
        started = []
        for other in others:
            slot = buf.at[other, chip, core]
            remote(slot, slot, zs.at[0], zr.at[other], {"shard": other}).wait_recv()
            for there in moves:
                started.append(
                    remote(
                        slot, slot, cs.at[other, there], cr.at[other, chip],
                        {"rep": 2 * there + core},
                    )
                )
                started[-1].start()
            started.append(remote(slot, slot, ps.at[other, chip], pr.at[other, chip], partner))
            started[-1].start()
        for other in others:
            for there in moves:
                slot = buf.at[other, there, core]
                remote(
                    slot, slot, cs.at[other, there], cr.at[other, there],
                    {"rep": 2 * there + core},
                ).wait_recv()
                started.append(
                    remote(slot, slot, ps.at[other, there], pr.at[other, there], partner)
                )
                started[-1].start()
        for other in others:
            for there in range(chips):
                slot = buf.at[other, there, 1 - core]
                remote(
                    slot, slot, ps.at[other, there], pr.at[other, there], partner
                ).wait_recv()
        for copy in started:
            copy.wait_send()
        matrix = buf[...].reshape(tall, wide).astype(f32)
        frobenius = jnp.sqrt(jnp.sum(matrix * matrix))
        cur[...] = (matrix / (frobenius + 1e-07)).astype(half)
        left = lax.div(shard * count, shards) < 2

        def finish_poly(gram):
            gram_ref[...] = gram.astype(half)
            gram = gram_ref[...]
            square = jnp.dot(gram, gram, preferred_element_type=f32)
            poly_ref[...] = (
                schulz_coeffs[1] * gram.astype(f32) + schulz_coeffs[2] * square
            ).astype(half)

        @pl.when(left)
        def _():
            @pl.loop(0, NS_STEPS)
            def _(turn):
                now = cur[...]
                finish_poly(
                    lax.dot_general(now, now, (((1,), (1,)), ((), ())), preferred_element_type=f32)
                )
                for q in range(wide // tall):
                    part = cur[:, q * tall : (q + 1) * tall]
                    cur[:, q * tall : (q + 1) * tall] = (
                        schulz_coeffs[0] * part.astype(f32)
                        + jnp.dot(poly_ref[...], part, preferred_element_type=f32)
                    ).astype(half)

        @pl.when(jnp.logical_not(left))
        def _():
            @pl.loop(0, NS_STEPS)
            def _(turn):
                gram = jnp.zeros((tall, tall), f32)
                for q in range(wide // tall):
                    part = cur[:, q * tall : (q + 1) * tall]
                    gram = gram + lax.dot_general(
                        part, part, (((0,), (0,)), ((), ())), preferred_element_type=f32
                    )
                finish_poly(gram)
                for q in range(wide // tall):
                    part = cur[:, q * tall : (q + 1) * tall]
                    cur[:, q * tall : (q + 1) * tall] = (
                        schulz_coeffs[0] * part.astype(f32)
                        + jnp.dot(part, poly_ref[...], preferred_element_type=f32)
                    ).astype(half)

        buf[...] = cur[...].reshape(buf.shape)

    if shards <= count:
        own_work()
    else:
        pl.when(lax.rem(shard * count, shards) == 0)(own_work)

    def back(number, other):
        return remote(
            buf.at[other, chip, core], ret.at[number, chip, core],
            zs2.at[other], zr2.at[number], {"shard": other},
        )

    for number in range(count):

        @pl.when(shard == owners[number])
        def _():
            for other in others:
                back(number, other).start()
            ret[number] = buf[shard]

    def spread(number):
        slot = ret.at[number, chip, core]
        copies = [
            remote(
                slot, slot, cs2.at[number, there], cr2.at[number, chip], {"rep": 2 * there + core}
            )
            for there in moves
        ]
        return copies + [remote(slot, slot, ps2.at[number, chip], pr2.at[number, chip], partner)]

    def relay(number, there):
        slot = ret.at[number, there, core]
        return remote(slot, slot, ps2.at[number, there], pr2.at[number, there], partner)

    for number in range(count):

        @pl.when(shard != owners[number])
        def _():
            back(number, owners[number]).wait_recv()
            for copy in spread(number):
                copy.start()

    for number in range(count):

        @pl.when(shard != owners[number])
        def _():
            for there in moves:
                slot = ret.at[number, there, core]
                remote(
                    slot, slot, cs2.at[number, there], cr2.at[number, there],
                    {"rep": 2 * there + core},
                ).wait_recv()
                relay(number, there).start()

    for number in range(count):

        @pl.when(shard != owners[number])
        def _():
            for there in range(chips):
                slot = ret.at[number, there, 1 - core]
                remote(
                    slot, slot, ps2.at[number, there], pr2.at[number, there], partner
                ).wait_recv()
            to_owner(number, shard).wait_send()
            for copy in spread(number):
                copy.wait_send()
            for there in moves:
                relay(number, there).wait_send()

        @pl.when(shard == owners[number])
        def _():
            for other in others:
                back(number, other).wait_send()


def orthogonal_rows(pieces, width):
    chips = lax.axis_size("rep") // 2
    shards = lax.axis_size("shard")
    half = jnp.bfloat16
    mats = jnp.stack(pieces).astype(half)
    mats = mats.reshape(len(pieces), chips, 2, mats.shape[1] // (2 * chips), width)
    tall = shards * pieces[0].shape[0]
    vmem = pl.BlockSpec(memory_space=pltpu.VMEM)
    dma = pltpu.SemaphoreType.DMA
    count = len(pieces)
    ret = pl.pallas_call(
        muon_kernel,
        out_shape=jax.ShapeDtypeStruct(mats.shape, half),
        in_specs=[vmem],
        out_specs=vmem,
        scratch_shapes=[
            pltpu.VMEM((shards,) + mats.shape[1:], half),
            pltpu.VMEM((tall, width), half),
            pltpu.VMEM((tall, tall), half),
            pltpu.VMEM((tall, tall), half),
            dma((count,)),
            dma((shards,)),
            dma((shards, chips)),
            dma((shards, chips)),
            dma((shards, chips)),
            dma((shards, chips)),
            dma((shards,)),
            dma((count,)),
            dma((count, chips)),
            dma((count, chips)),
            dma((count, chips)),
            dma((count, chips)),
        ],
        compiler_params=pltpu.CompilerParams(
            collective_id=2, has_side_effects=True, vmem_limit_bytes=60 * 1024 * 1024
        ),
    )(mats)
    return ret.reshape(count, pieces[0].shape[0], width)


def muon_apply(weight, orth, full_shape):
    factor = 0.2 * math.sqrt(max(full_shape[0], full_shape[1]))
    return weight - muon_rate * (factor * orth.astype(jnp.float32) + decay_rate * weight)


def adam_apply(param, grad, state):
    first = beta_first * state[0] + (1.0 - beta_first) * grad
    second = beta_second * state[1] + (1.0 - beta_second) * grad * grad
    first_hat = first / (1.0 - beta_first**ADAM_STEP)
    second_hat = second / (1.0 - beta_second**ADAM_STEP)
    updated = param - adam_rate * (
        first_hat / (jnp.sqrt(second_hat) + adam_eps) + decay_rate * param
    )
    return (updated, jnp.stack([first, second]))


MESH = pl.DeviceIdType.MESH


def places():
    rep = lax.axis_index("rep")
    shard = lax.axis_index("shard")
    core = lax.rem(rep, 2)
    chip = lax.div(rep, 2)
    chips = lax.axis_size("rep") // 2
    shards = lax.axis_size("shard")
    return rep, shard, core, chip, chips, shards


def greet_peers(core, chip, shard, chips, shards):
    barrier = pltpu.get_barrier_semaphore()
    peers = [{"rep": 2 * chip + 1 - core}]
    for step in range(1, chips):
        peers.append({"rep": 2 * lax.rem(chip + step, chips) + core})
    for step in range(1, shards):
        peers.append({"shard": lax.rem(shard + step, shards)})
    for peer in peers:
        pl.semaphore_signal(barrier, inc=1, device_id=peer, device_id_type=MESH)
    pl.semaphore_wait(barrier, len(peers))


def remote(src, dst, send, recv, peer):
    return pltpu.make_async_remote_copy(
        src_ref=src, dst_ref=dst, send_sem=send, recv_sem=recv, device_id=peer, device_id_type=MESH
    )


def gather_kernel(in_ref, out_ref, all_in, all_out, own_sem, zs, zr, cs, cr, ps, pr):
    rep, shard, core, chip, chips, shards = places()
    partner = {"rep": 2 * chip + 1 - core}
    pairs = ((in_ref, all_in), (out_ref, all_out))
    own = []
    for a, (src, dst) in enumerate(pairs):
        own.append(pltpu.make_async_copy(src, dst.at[shard], own_sem.at[a]))
        own[-1].start()
    greet_peers(core, chip, shard, chips, shards)
    started = []
    for a, (src, dst) in enumerate(pairs):
        for step in range(1, shards):
            other = lax.rem(shard + step, shards)
            copy = remote(
                src.at[chip, core], dst.at[shard, chip, core],
                zs.at[a, other], zr.at[a, shard], {"shard": other},
            )
            copy.start()
            started.append(copy)
    for a, (src, dst) in enumerate(pairs):
        for step in range(1, shards):
            other = lax.rem(shard + step, shards)
            slot = dst.at[other, chip, core]
            remote(slot, slot, zs.at[a, other], zr.at[a, other], {"shard": other}).wait_recv()
            for move in range(1, chips):
                there = lax.rem(chip + move, chips)
                copy = remote(
                    slot, slot, cs.at[a, other, there], cr.at[a, other, chip],
                    {"rep": 2 * there + core},
                )
                copy.start()
                started.append(copy)
            copy = remote(slot, slot, ps.at[a, other, chip], pr.at[a, other, chip], partner)
            copy.start()
            started.append(copy)
    for a, (src, dst) in enumerate(pairs):
        for step in range(1, shards):
            other = lax.rem(shard + step, shards)
            for move in range(1, chips):
                there = lax.rem(chip + move, chips)
                slot = dst.at[other, there, core]
                remote(
                    slot, slot, cs.at[a, other, there], cr.at[a, other, there],
                    {"rep": 2 * there + core},
                ).wait_recv()
                copy = remote(slot, slot, ps.at[a, other, there], pr.at[a, other, there], partner)
                copy.start()
                started.append(copy)
    for a, (src, dst) in enumerate(pairs):
        for step in range(1, shards):
            other = lax.rem(shard + step, shards)
            for there in range(chips):
                slot = dst.at[other, there, 1 - core]
                remote(
                    slot, slot, ps.at[a, other, there], pr.at[a, other, there], partner
                ).wait_recv()
    for copy in started:
        copy.wait_send()
    for copy in own:
        copy.wait()


def gather_rows(in_half, out_half):
    chips = lax.axis_size("rep") // 2
    shards = lax.axis_size("shard")

    def split(rows):
        return rows.reshape(chips, 2, rows.shape[0] // (2 * chips), rows.shape[1])

    parts = [split(in_half), split(out_half)]
    vmem = pl.BlockSpec(memory_space=pltpu.VMEM)
    dma = pltpu.SemaphoreType.DMA
    whole = pl.pallas_call(
        gather_kernel,
        out_shape=[jax.ShapeDtypeStruct((shards,) + p.shape, p.dtype) for p in parts],
        in_specs=[vmem, vmem],
        out_specs=[vmem, vmem],
        scratch_shapes=[
            dma((2,)),
            dma((2, shards)),
            dma((2, shards)),
            dma((2, shards, chips)),
            dma((2, shards, chips)),
            dma((2, shards, chips)),
            dma((2, shards, chips)),
        ],
        compiler_params=pltpu.CompilerParams(
            collective_id=0, has_side_effects=True, vmem_limit_bytes=60 * 1024 * 1024
        ),
    )(*parts)
    return [
        w.reshape(shards * half.shape[0], half.shape[1])
        for w, half in zip(whole, (in_half, out_half))
    ]


def reduce_kernel(
    gin, gout, small, fin, fout, ftiny,
    r0i, r0o, a1i, a1o, r1i, r1o, a2i, a2o, r2i, r2o, t0, t1, t2,
    s0, v0, s1, v1, s2, v2, s3, v3, s4, v4,
):
    rep, shard, core, chip, chips, shards = places()
    partner = {"rep": 2 * chip + 1 - core}
    sources = (gin, gout)
    first = (r0i, r0o)
    sums = (a1i, a1o)
    second = (r1i, r1o)
    planes = (a2i, a2o)
    third = (r2i, r2o)
    finals = (fin, fout)
    f32 = jnp.float32
    started = []

    def go(copy):
        copy.start()
        started.append(copy)

    t0[core] = small[...]
    greet_peers(core, chip, shard, chips, shards)
    go(remote(small, t0.at[core], s0.at[2, 0], v0.at[2, 0], partner))
    order = [lax.rem(chip + move, chips) for move in range(1, chips)] + [chip]
    for there in order:
        for a in range(2):
            go(
                remote(
                    sources[a].at[:, there, 1 - core], first[a].at[there],
                    s0.at[a, there], v0.at[a, there], partner,
                )
            )
    remote(small, t0.at[1 - core], s0.at[2, 0], v0.at[2, 0], partner).wait_recv()
    t1[chip] = t0[0] + t0[1]
    for there in order[:-1]:
        peer = {"rep": 2 * there + core}
        go(remote(t1.at[chip], t1.at[chip], s1.at[2, there], v1.at[2, chip], peer))
    for number, there in enumerate(order):
        for a in range(2):
            remote(
                first[a].at[there], first[a].at[there], s0.at[a, there], v0.at[a, there], partner
            ).wait_recv()
            sums[a][there] = (
                sources[a][:, there, core].astype(f32) + first[a][there].astype(f32)
            ).astype(jnp.bfloat16)
            if number < chips - 1:
                go(
                    remote(
                        sums[a].at[there], second[a].at[chip],
                        s1.at[a, there], v1.at[a, chip], {"rep": 2 * there + core},
                    )
                )
    for there in order[:-1]:
        peer = {"rep": 2 * there + core}
        remote(t1.at[there], t1.at[there], s1.at[2, there], v1.at[2, there], peer).wait_recv()
    total = t1[0]
    for there in range(1, chips):
        total = total + t1[there]
    t2[shard] = total
    zorder = [lax.rem(shard + step, shards) for step in range(1, shards)]
    for other in zorder:
        go(remote(t2.at[shard], t2.at[shard], s2.at[2, other], v2.at[2, shard], {"shard": other}))
    for a in range(2):
        for there in order[:-1]:
            remote(
                second[a].at[there], second[a].at[there], s1.at[a, there], v1.at[a, there],
                {"rep": 2 * there + core},
            ).wait_recv()
        for other in zorder + [shard]:
            part = sums[a][chip, other].astype(f32)
            for there in order[:-1]:
                part = part + second[a][there, other].astype(f32)
            planes[a][other] = part.astype(jnp.bfloat16)
        for other in zorder:
            go(
                remote(
                    planes[a].at[other], third[a].at[shard],
                    s2.at[a, other], v2.at[a, shard], {"shard": other},
                )
            )
    for a in range(2):
        part = planes[a][shard].astype(f32)
        for other in zorder:
            remote(
                third[a].at[other], third[a].at[other], s2.at[a, other], v2.at[a, other],
                {"shard": other},
            ).wait_recv()
            part = part + third[a][other].astype(f32)
        finals[a][chip, core] = part.astype(jnp.bfloat16)
        slot = finals[a].at[chip, core]
        for there in order[:-1]:
            go(remote(slot, slot, s3.at[a, there], v3.at[a, chip], {"rep": 2 * there + core}))
        go(remote(slot, slot, s4.at[a, chip], v4.at[a, chip], partner))
    for other in zorder:
        remote(
            t2.at[other], t2.at[other], s2.at[2, other], v2.at[2, other], {"shard": other}
        ).wait_recv()
    total = t2[0]
    for other in range(1, shards):
        total = total + t2[other]
    ftiny[...] = total
    for a in range(2):
        for there in order[:-1]:
            slot = finals[a].at[there, core]
            remote(
                slot, slot, s3.at[a, there], v3.at[a, there], {"rep": 2 * there + core}
            ).wait_recv()
            go(remote(slot, slot, s4.at[a, there], v4.at[a, there], partner))
    for a in range(2):
        for there in range(chips):
            slot = finals[a].at[there, 1 - core]
            remote(slot, slot, s4.at[a, there], v4.at[a, there], partner).wait_recv()
    for copy in started:
        copy.wait_send()


def reduce_grads(grad_in, grad_out, small):
    chips = lax.axis_size("rep") // 2
    shards = lax.axis_size("shard")
    half = jnp.bfloat16

    def split(grad):
        rows = grad.shape[0] // (shards * chips * 2)
        return grad.reshape(shards, chips, 2, rows, grad.shape[1])

    parts = [split(grad_in), split(grad_out)]
    tails = [p.shape[3:] for p in parts]
    vmem = pl.BlockSpec(memory_space=pltpu.VMEM)
    dma = pltpu.SemaphoreType.DMA
    big = [pltpu.VMEM((chips, shards) + t, half) for t in tails]
    mid = [pltpu.VMEM((shards,) + t, half) for t in tails]
    fin, fout, tiny = pl.pallas_call(
        reduce_kernel,
        out_shape=[jax.ShapeDtypeStruct((chips, 2) + t, half) for t in tails]
        + [jax.ShapeDtypeStruct(small.shape, small.dtype)],
        in_specs=[vmem] * 3,
        out_specs=[vmem] * 3,
        scratch_shapes=big
        + big
        + big
        + mid
        + mid
        + [pltpu.VMEM((n,) + small.shape, small.dtype) for n in (2, chips, shards)]
        + [dma((3, chips))] * 4
        + [dma((3, shards))] * 2
        + [dma((2, chips))] * 4,
        compiler_params=pltpu.CompilerParams(
            collective_id=1, has_side_effects=True, vmem_limit_bytes=60 * 1024 * 1024
        ),
    )(*parts, small)
    return (
        fin.reshape(grad_in.shape[0] // shards, grad_in.shape[1]),
        fout.reshape(grad_out.shape[0] // shards, grad_out.shape[1]),
        tiny,
    )


def pack_small(arrays):
    flat = jnp.concatenate([a.reshape(-1) for a in arrays])
    rows = -(-flat.shape[0] // 1024) * 8
    return jnp.pad(flat, (0, rows * 128 - flat.shape[0])).reshape(rows, 128)


def unpack_small(packed, arrays):
    flat = packed.reshape(-1)
    pieces = []
    start = 0
    for a in arrays:
        pieces.append(flat[start : start + a.size].reshape(a.shape))
        start += a.size
    return pieces


def local(
    tokens,
    cotangent,
    block_fill,
    block_start,
    in_weight,
    out_weight,
    in_moment,
    out_moment,
    norm_gain,
    gate_gain,
    conv_params,
    head_params,
    adam_norm,
    adam_gate,
    adam_conv,
    adam_head,
):
    shards = lax.axis_size("shard")
    replicas = lax.axis_size("rep")
    in_half = in_weight.astype(jnp.bfloat16)
    out_half = out_weight.astype(jnp.bfloat16)
    whole_in, whole_out = gather_rows(in_half, out_half)
    results = device_pass(
        tokens,
        cotangent,
        block_fill,
        block_start,
        whole_in,
        whole_out,
        whole_in,
        whole_out,
        norm_gain,
        gate_gain,
        conv_params,
        head_params,
    )
    activations, input_grad, grad_in, grad_out, grad_norm, grad_gate, grad_conv, grad_head = results
    scale = 1.0 / math.sqrt(tokens.shape[0] * shards * replicas)
    smalls = [scale * grad_norm, scale * grad_gate, scale * grad_conv, scale * grad_head]
    half_in, half_out, tiny = reduce_grads(
        (scale * grad_in).astype(jnp.bfloat16),
        (scale * grad_out).astype(jnp.bfloat16),
        pack_small(smalls),
    )
    grad_norm, grad_gate, grad_conv, grad_head = unpack_small(tiny, smalls)
    part_in = half_in.astype(jnp.float32)
    part_out = half_out.astype(jnp.float32)
    new_in_moment = momentum_keep * in_moment + part_in
    new_out_moment = momentum_keep * out_moment + part_out
    width_inner = gate_gain.shape[0]
    rows_here = in_weight.shape[0]
    rows_all = rows_here * shards
    folds = new_out_moment.shape[0] // rows_here
    tail = in_weight.shape[1] - 2 * width_inner
    folded = jnp.transpose(
        new_out_moment.reshape(folds, rows_here, new_out_moment.shape[1]), (1, 0, 2)
    ).reshape(rows_here, width_inner)
    pieces = [
        new_in_moment[:, :width_inner],
        new_in_moment[:, width_inner : 2 * width_inner],
        jnp.pad(new_in_moment[:, 2 * width_inner :], ((0, 0), (0, width_inner - tail))),
        folded,
    ]
    orths = orthogonal_rows(pieces, width_inner)
    unfolded = jnp.transpose(
        orths[3].reshape(rows_here, folds, new_out_moment.shape[1]), (1, 0, 2)
    ).reshape(new_out_moment.shape)
    owned = [orths[0], orths[1], orths[2][:, :tail], unfolded]
    full_shapes = [
        (rows_all, width_inner),
        (rows_all, width_inner),
        (rows_all, tail),
        (new_out_moment.shape[0] * shards, new_out_moment.shape[1]),
    ]
    new_in_weight = jnp.concatenate(
        [
            muon_apply(in_weight[:, :width_inner], owned[0], full_shapes[0]),
            muon_apply(in_weight[:, width_inner : 2 * width_inner], owned[1], full_shapes[1]),
            muon_apply(in_weight[:, 2 * width_inner :], owned[2], full_shapes[2]),
        ],
        1,
    )
    new_out_weight = muon_apply(out_weight, owned[3], full_shapes[3])
    new_norm, state_norm = adam_apply(norm_gain, grad_norm, adam_norm)
    new_gate, state_gate = adam_apply(gate_gain, grad_gate, adam_gate)
    new_conv, state_conv = adam_apply(conv_params, grad_conv, adam_conv)
    new_head, state_head = adam_apply(head_params, grad_head, adam_head)
    return (
        activations,
        input_grad,
        part_in,
        part_out,
        grad_norm,
        grad_gate,
        grad_conv,
        grad_head,
        new_in_weight,
        new_out_weight,
        new_in_moment,
        new_out_moment,
        new_norm,
        new_gate,
        new_conv,
        new_head,
        state_norm,
        state_gate,
        state_conv,
        state_head,
    )


def solution(mesh):
    return jax.shard_map(
        local,
        mesh=mesh,
        in_specs=(
            P(("rep", "shard"), None),
            P(("rep", "shard"), None),
            P(("rep", "shard")),
            P(("rep", "shard")),
            P("shard", None),
            P("shard", None),
            P("shard", None),
            P("shard", None),
            P(),
            P(),
            P(),
            P(),
            P(),
            P(),
            P(),
            P(),
        ),
        out_specs=(
            P(("rep", "shard"), None),
            P(("rep", "shard"), None),
            P("shard", None),
            P("shard", None),
            P(),
            P(),
            P(),
            P(),
            P("shard", None),
            P("shard", None),
            P("shard", None),
            P("shard", None),
            P(),
            P(),
            P(),
            P(),
            P(),
            P(),
            P(),
            P(),
        ),
        check_vma=False,
    )
```

profile of v0, /device:TPU:0, one launch (start us, length us, event | category | flops | bytes accessed | tf_op | source)
XLA Modules:
  0.0 175.9 jit_solution(4506601000379250457)
XLA Ops:
  0.7 1.4 convert_element_type.81
  2.1 1.1 copy.73
  3.2 0.7 convert_element_type.82
  3.9 32.8 %shard_map.311 = (bf16[4,4,2,16,2320]{4,3,2,1,0:T(8,128)(2,1)}, bf16[4,4,2,32,512]{4,3,2,1,0:T(8,128)(2,1)}) custom-call(bf16[4,2,16,2320]{3,2,1,0:T(8,128)(2,1)} %bitcast.131, bf16[4,2,32,512]{3,2,1,0:T(8,128)(2,1)} %bitcast.140), custom_call_target="tpu_custom_call" | custom-call | tf_op jit(solution)/shard_map/pallas_call | solution.py:463
  37.0 2.8 %fusion.62 = f32[256,2320]{0,1:T(8,128)S(1)} fusion(bf16[512,2320]{1,0:T(8,128)(2,1)} %bitcast.129, bf16[256,512]{1,0:T(8,128)(2,1)S(1)} %copy-done.5, f32[512]{0:T(512)S(1)} %copy-done.20, f32[256]{0:T(256)S(1)} %fusion.102), kind=kOutput, calls=%fused_computation.108 | convolution fusion | flops 608698368 | bytes 5016576 | tf_op jit(solution)/shard_map/dot_general | solution.py:95
  40.2 0.7 copy-done.16
  41.2 2.3 %fusion.30 = (f32[256,1280]{0,1:T(8,128)S(1)}, f32[256,1280]{0,1:T(8,128)S(1)}) fusion(f32[256]{0:T(256)S(1)} %get-tuple-element.164, f32[253,1280]{0,1:T(8,128)S(1)} %slice.204, f32[1280]{0:T(1024)S(1)} %get-tuple-element.103, f32[256]{0:T(256)S(1)} %get-tuple-element.165, f32[254,1280]{0,1:T(8,128)S(1)} %slice.203, f32[1280]{0:T(1024)S(1)} %get-tuple-element.100, ...), kind=kLoop, calls=%fused_computation.40 | loop fusion | flops 4915200 | bytes 7862272 | tf_op jit(solution)/shard_map/jvp(jit(silu))/mul | solution.py:51
  44.4 2.8 %fusion.25 = f32[256,16,64]{0,2,1:T(8,128)S(1)} fusion(f32[256,256]{1,0:T(8,128)S(1)} %fusion.56, f32[16,256]{1,0:T(8,128)S(1)} %fusion.52, pred[256,256]{1,0:T(8,128)(4,1)S(1)} %fusion.53, f32[256,16,64]{0,2,1:T(8,128)S(1)} %bitcast.141, f32[16]{0:T(128)S(1)} %get-tuple-element.160, f32[256,16]{0,1:T(8,128)S(1)} %compare_select_fusion.2), kind=kOutput, calls=%fused_computation.28 | convolution fusion | flops 407633920 | bytes 2457664 | tf_op jit(solution)/shard_map/jvp(hts,shp->thp)/dot_general | solution.py:66
  47.2 0.4 multiply_reduce_fusion.9
  47.5 0.5 copy-done.6
  48.1 0.4 copy-done.10
  48.5 1.5 fusion.32
  50.0 0.6 multiply_reduce_fusion.6
  50.6 1.0 multiply_reduce_fusion.5
  51.6 2.3 %multiply_reduce_fusion.7 = (f32[256,16]{0,1:T(8,128)S(1)}, f32[256,16,64]{0,2,1:T(8,128)S(1)}) fusion(f32[256,1280]{0,1:T(8,128)S(1)} %get-tuple-element.128, f32[256,16]{0,1:T(8,128)S(1)} %compare_select_fusion.2, f32[256,16,64]{0,2,1:T(8,128)S(1)} %bitcast.137, f32[16]{0:T(128)S(1)} %get-tuple-element.160, f32[16,64,256]{2,1,0:T(8,128)S(1)} %bitcast.138, ...), kind=kOutput, calls=%fused_computation.55 | convolution fusion | flops 408154112 | bytes 4588032 | tf_op jit(solution)/shard_map/transpose(jvp(hts,shp->thp))/dot_general | solution.py:66
  53.9 4.8 %fusion.8 = (f32[16,256]{1,0:T(8,128)S(1)}, f32[16,256]{1,0:T(8,128)S(1)}, f32[256,256]{1,0:T(8,128)S(1)}) fusion(f32[256,256]{1,0:T(8,128)S(1)} %fusion.56, f32[16,256]{1,0:T(8,128)S(1)} %fusion.52, pred[256,256]{1,0:T(8,128)(4,1)S(1)} %fusion.53, f32[16,64,256]{2,1,0:T(8,128)S(1)} %bitcast.139, f32[256,16,64]{0,2,1:T(8,128)S(1)} %bitcast.142, ...), kind=kOutput, calls=%fused_computation.10 | convolution fusion | flops 414375936 | bytes 2752512 | tf_op jit(solution)/shard_map/transpose(jvp(hts,shp->thp))/dot_general | solution.py:66
  59.2 0.8 multiply_reduce_fusion.4
  60.1 1.4 multiply_reduce_fusion.3
  61.4 0.6 slice_multiply_fusion
  62.0 0.6 slice_multiply_fusion.1
  62.6 0.6 slice_multiply_fusion.2
  63.2 0.8 multiply_reduce_fusion.1
  64.3 0.6 copy-done.2
  64.9 1.8 fusion.42
  66.6 0.6 multiply_multiply_fusion.7
  67.2 0.9 fusion
  68.1 2.7 %copy.75 = bf16[512,2320]{1,0:T(8,128)(2,1)} copy(bf16[512,2320]{0,1:T(8,128)(2,1)S(1)} %fusion) | data formatting | bytes 4751360 | tf_op jit(solution)/shard_map/convert_element_type | solution.py:702
  70.8 2.5 %multiply_convert_fusion = bf16[1024,512]{1,0:T(8,128)(2,1)} fusion(bf16[256,512]{1,0:T(8,128)(2,1)} %param.17, pred[256]{0:T(512)(128)(4,1)S(1)} %fusion.100, f32[256,1024]{0,1:T(8,128)S(1)} %get-tuple-element.127, f32[1024]{0:T(1024)S(1)} %copy-done.18, f32[256]{0:T(256)S(1)} %fusion.103), kind=kOutput, calls=%fused_computation.12 | convolution fusion | flops 270401536 | bytes 2364672 | tf_op jit(solution)/shard_map/dot_general | solution.py:106
  73.7 0.6 fusion.76.small
  74.3 44.8 %shard_map.312 = (bf16[4,2,16,2320]{3,2,1,0:T(8,128)(2,1)}, bf16[4,2,32,512]{3,2,1,0:T(8,128)(2,1)}, f32[64,128]{1,0:T(8,128)}) custom-call(bf16[4,4,2,16,2320]{4,3,2,1,0:T(8,128)(2,1)} %bitcast.126, bf16[4,4,2,32,512]{4,3,2,1,0:T(8,128)(2,1)} %bitcast.127, f32[64,128]{1,0:T(8,128)} %fusion.76.small), custom_call_target="tpu_custom_call" | custom-call | tf_op jit(solution)/shard_map/pallas_call | solution.py:619
  119.2 2.1 %fusion.110 = (bf16[256,512]{1,0:T(8,128)(2,1)S(1)}, f32[256,512]{1,0:T(8,128)}, f32[256,512]{1,0:T(8,128)}) fusion(f32[256,512]{1,0:T(8,128)S(1)} %copy-done.12, bf16[4,2,32,512]{3,2,1,0:T(8,128)(2,1)} %get-tuple-element.28), kind=kLoop, calls=%fused_computation.213 | loop fusion | flops 524288 | bytes 2097152 | tf_op jit(solution)/shard_map/convert.8
  121.9 0.4 copy.88
  122.3 2.9 %fusion.109 = (bf16[128,2320]{0,1:T(8,128)(2,1)S(1)}, f32[128,2320]{0,1:T(8,128)}) fusion(f32[128,2320]{0,1:T(8,128)S(1)} %copy.88, f32[128,2320]{0,1:T(8,128)} %param.22), kind=kLoop, calls=%fused_computation.212 | loop fusion | flops 890880 | bytes 4157440 | tf_op jit(solution)/shard_map/convert.16
  125.7 1.1 pad_maximum_fusion.1.mats
  126.8 37.6 %shard_map.313 = bf16[4,4,2,16,1024]{4,3,2,1,0:T(8,128)(2,1)} custom-call(bf16[4,4,2,16,1024]{4,3,2,1,0:T(8,128)(2,1)} %pad_maximum_fusion.1.mats), custom_call_target="tpu_custom_call" | custom-call | tf_op jit(solution)/shard_map/pallas_call | solution.py:314
  164.5 1.3 convert_multiply_fusion.4
  165.8 0.4 mul.839
  167.0 0.4 copy-done.13
  167.4 1.2 fusion.43
  168.7 0.6 multiply_subtract_fusion.5
  169.3 0.6 fusion.91
  171.0 1.1 pad_maximum_fusion
  172.1 0.7 multiply_subtract_fusion.3
  172.8 0.6 fusion.104
  173.4 0.6 pad_maximum_fusion.4
  174.0 0.6 pad_maximum_fusion.3
  174.6 0.6 copy.89
  175.3 0.6 copy.90
  (130 shorter events, 5.8 us)
Async XLA Ops:
  0.7 2.5 %copy-start.8 = (f32[256,512]{1,0:T(8,128)S(1)}, f32[256,512]{1,0:T(8,128)}, u32[]{:S(2)}) copy-start(f32[256,512]{1,0:T(8,128)} %param.21) | copy-start | bytes 1572868
  2.1 34.7 %copy-start.32 = (s32[2]{0:T(128)S(1)}, s32[2]{0:T(128)}, u32[]{:S(2)}) copy-start(s32[2]{0:T(128)} %param.18) | copy-start | bytes 28
  2.1 34.7 %copy-start.5 = (bf16[256,512]{1,0:T(8,128)(2,1)S(1)}, bf16[256,512]{1,0:T(8,128)(2,1)}, u32[]{:S(2)}) copy-start(bf16[256,512]{1,0:T(8,128)(2,1)} %param.16) | copy-start | bytes 786436
  2.1 34.9 %copy-start.20 = (f32[512]{0:T(512)S(1)}, f32[512]{0:T(512)}, u32[]{:S(2)}) copy-start(f32[512]{0:T(512)} %param.24) | copy-start | bytes 6148
  36.8 34.0 %copy-start.27 = (pred[256]{0:T(512)(128)(4,1)}, pred[256]{0:T(512)(128)(4,1)S(1)}, u32[]{:S(2)}) copy-start(pred[256]{0:T(512)(128)(4,1)S(1)} %fusion.100) | copy-start | bytes 772
  37.0 2.9 %copy-start.33 = (s32[2]{0:T(128)S(1)}, s32[2]{0:T(128)}, u32[]{:S(2)}) copy-start(s32[2]{0:T(128)} %param.19) | copy-start | bytes 28
  40.2 0.8 copy-start.16
  41.2 2.6 %copy-start.25 = (f32[3,16]{1,0:T(4,128)S(1)}, f32[3,16]{1,0:T(4,128)}, u32[]{:S(2)}) copy-start(f32[3,16]{1,0:T(4,128)} %param.27) | copy-start | bytes 580
  47.1 1.0 copy-start.6
  47.1 1.3 copy-start.10
  47.1 1.3 copy-start.18
  48.4 1.5 copy-start.3
  63.2 1.7 copy-start.2
  74.3 44.8 %copy-start.12 = (f32[256,512]{1,0:T(8,128)S(1)}, f32[256,512]{1,0:T(8,128)}, u32[]{:S(2)}) copy-start(f32[256,512]{1,0:T(8,128)} %param.23) | copy-start | bytes 1572868
  119.2 2.6 %copy-start.11 = (bf16[4,2,16,2320]{3,2,1,0:T(8,128)(2,1)S(1)}, bf16[4,2,16,2320]{3,2,1,0:T(8,128)(2,1)}, u32[]{:S(2)}) copy-start(bf16[4,2,16,2320]{3,2,1,0:T(8,128)(2,1)} %get-tuple-element.27) | copy-start | bytes 1781764
  122.3 2.9 %copy-start.1 = (f32[128,2320]{0,1:T(8,128)}, f32[128,2320]{0,1:T(8,128)S(1)}, u32[]{:S(2)}) copy-start(f32[128,2320]{0,1:T(8,128)S(1)} %copy.88) | copy-start | bytes 3563524
  165.7 1.0 copy-start.4
  165.8 1.0 copy-start.7
  165.8 1.2 copy-start.9
  165.8 1.2 copy-start.21
  165.8 1.2 copy-start.28
  165.8 1.2 copy-start.29
  166.3 1.1 copy-start.13
  167.4 1.2 copy-start.14
  167.4 1.2 copy-start.30
  167.4 1.3 copy-start.22
  167.4 1.9 %copy-start.23 = (f32[2,1024]{1,0:T(2,128)S(1)}, f32[2,1024]{1,0:T(2,128)}, u32[]{:S(2)}) copy-start(f32[2,1024]{1,0:T(2,128)} %param.29) | copy-start | bytes 24580
  167.4 2.5 %copy-start.31 = (f32[2,3,16]{2,0,1:T(2,128)S(1)}, f32[2,3,16]{2,0,1:T(2,128)}, u32[]{:S(2)}) copy-start(f32[2,3,16]{2,0,1:T(2,128)} %param.31) | copy-start | bytes 1156
  167.4 2.7 %slice-start = ((bf16[4,4,2,16,1024]{4,3,2,1,0:T(8,128)(2,1)}), bf16[1,4,2,16,1024]{4,3,2,1,0:T(8,128)(2,1)S(1)}, s32[]{:S(2)}) async-start(bf16[4,4,2,16,1024]{4,3,2,1,0:T(8,128)(2,1)} %shard_map.313), calls=%async_computation | async-start | bytes 524288 | tf_op jit(solution)/shard_map/slice | solution.py:729
  168.6 1.7 copy-start
  169.9 2.1 %copy-start.15 = (f32[5,1280]{1,0:T(8,128)}, f32[5,1280]{1,0:T(8,128)S(1)}, u32[]{:S(2)}) copy-start(f32[5,1280]{1,0:T(8,128)S(1)} %reshape.435) | copy-start | bytes 76804
  170.1 2.7 %copy-start.24 = (f32[3,16]{1,0:T(4,128)}, f32[3,16]{1,0:T(4,128)S(1)}, u32[]{:S(2)}) copy-start(f32[3,16]{1,0:T(4,128)S(1)} %get-tuple-element.105) | copy-start | bytes 580
  170.9 1.1 copy-start.19
  170.9 1.2 copy-start.17
  170.9 1.8 %copy-start.26 = (f32[3,16]{1,0:T(4,128)S(1)}, f32[3,16]{1,0:T(4,128)}, u32[]{:S(2)}) copy-start(f32[3,16]{1,0:T(4,128)} %param.27) | copy-start | bytes 580
where the time goes:
time: 176 us
  Pallas kernels  115 us (65%)
  other arithmetic  26.4 us (15%)
  matrix products  21.3 us (12%)
  local copies, waits for them, and re-layouts  11.6 us (7%)
    pallas_call x1, Pallas kernels, reduce_grads(): pl.pallas_call(reduce_kernel, out_shape=[jax.ShapeDtypeStruct((chips, 2)...  44.8 us
    pallas_call x1, Pallas kernels, orthogonal_rows(): pl.pallas_call(muon_kernel, out_shape=jax.ShapeDtypeStruct(mats.shape, ha...  37.6 us
    pallas_call x1, Pallas kernels, gather_rows(): pl.pallas_call(gather_kernel, out_shape=[jax.ShapeDtypeStruct((shards,) +...  32.8 us
    dot_general x3, matrix products, mixer(): jnp.einsum('hts,shp->thp', decay * scores[None], weighted, precision=ssd_...  9.9 us
    another operation x3, other arithmetic  5.21 us
    unnamed x73, local copies, waits for them, and re-layouts  5.21 us

commit v1 on v0

v1 whole, which is shorter than its diff:
```python
import functools
import math

import jax
import jax.numpy as jnp
from jax import lax
from jax.experimental import pallas as pl
from jax.experimental.pallas import tpu as pltpu
from jax.sharding import PartitionSpec as P

NS_STEPS = 5
ADAM_STEP = 3


ssd_precision = lax.Precision.HIGH
norm_eps = 1e-05
schulz_coeffs = (3.4445, -4.775, 2.0315)
momentum_keep = 0.95
muon_rate = 0.05
adam_rate = 0.2
beta_first = 0.9
beta_second = 0.95
decay_rate = 0.1
adam_eps = 1e-08


def pre_norm(base, gain):
    return base * lax.rsqrt(jnp.mean(base * base, -1, keepdims=True) + norm_eps) * gain


def mixer(proj, conv_params, head_params, gate_gain, starts):
    total = proj.shape[0]
    blocks = starts.shape[0]
    length = total // blocks
    width_inner = gate_gain.shape[0]
    heads = head_params.shape[1]
    head_size = width_inner // heads
    taps = conv_params.shape[0] - 1
    channels = conv_params.shape[1]
    state_size = (channels - width_inner) // 2
    gate_in = proj[:, :width_inner]
    conv_in = proj[:, width_inner : width_inner + channels]
    dt_raw = proj[:, width_inner + channels :]
    seq_block = jnp.cumsum(starts)
    seq_token = jnp.repeat(seq_block, length)
    summed = conv_params[taps] + conv_params[taps - 1] * conv_in
    for offset in range(1, taps):
        moved = jnp.concatenate([jnp.zeros((offset, channels), jnp.float32), conv_in[:-offset]], 0)
        moved_seq = jnp.concatenate([jnp.full((offset,), -1, jnp.int32), seq_token[:-offset]], 0)
        same_seq = (moved_seq == seq_token).astype(jnp.float32)
        summed = summed + conv_params[taps - 1 - offset] * moved * same_seq[:, None]
    activated = jax.nn.silu(summed)
    values = activated[:, :width_inner].reshape(total, heads, head_size)
    b_input = activated[:, width_inner : width_inner + state_size]
    c_input = activated[:, width_inner + state_size :]
    step_size = jax.nn.softplus(dt_raw + head_params[0])
    rates = -jnp.exp(head_params[1])
    lower = jnp.tril(jnp.ones((total, total), jnp.bool_))
    mask = jnp.logical_and(lower, seq_token[:, None] == seq_token[None, :])
    columns = jnp.einsum(
        "ts,sh->ht", lower.astype(jnp.float32), step_size * rates, precision=lax.Precision.HIGHEST
    )
    spread = columns[:, :, None] - columns[:, None, :]
    decay = jnp.where(mask, jnp.exp(jnp.where(mask, spread, 0.0)), 0.0)
    scores = jnp.dot(c_input, b_input.T, precision=ssd_precision)
    weighted = values * step_size[:, :, None]
    outputs = jnp.einsum(
        "hts,shp->thp", decay * scores[None], weighted, precision=ssd_precision
    )
    outputs = outputs + head_params[2][None, :, None] * values
    gated = outputs.reshape(total, width_inner) * jax.nn.silu(gate_in)
    return gated * lax.rsqrt(jnp.mean(gated * gated, -1, keepdims=True) + norm_eps) * gate_gain


def device_pass(
    tokens,
    cotangent,
    fill,
    starts,
    fwd_in,
    fwd_out,
    back_in,
    back_out,
    norm_gain,
    gate_gain,
    conv_params,
    head_params,
):
    total = tokens.shape[0]
    length = total // fill.shape[0]
    position = jnp.arange(total, dtype=jnp.int32) % length
    live = position < jnp.repeat(fill, length)
    base = tokens.astype(jnp.float32)
    normed, norm_back = jax.vjp(pre_norm, base, norm_gain)
    normed16 = normed.astype(jnp.bfloat16)
    proj = jnp.dot(normed16, fwd_in, preferred_element_type=jnp.float32)

    def mix_piece(proj_in, conv_in, head_in, gain_in):
        return mixer(proj_in, conv_in, head_in, gain_in, starts)

    mixed, mixer_back = jax.vjp(mix_piece, proj, conv_params, head_params, gate_gain)
    mixed16 = mixed.astype(jnp.bfloat16)
    branch = jnp.dot(mixed16, fwd_out, preferred_element_type=jnp.float32)
    activations = jnp.where(live[:, None], base + branch, 0.0).astype(jnp.bfloat16)
    live_cot = jnp.where(live[:, None], cotangent, jnp.zeros_like(cotangent))
    d_mixed = jnp.dot(live_cot, back_out.T, preferred_element_type=jnp.float32)
    grad_out = jnp.dot(mixed16.T, live_cot, preferred_element_type=jnp.float32)
    d_proj, grad_conv, grad_head, grad_gate = mixer_back(d_mixed)
    d_proj16 = d_proj.astype(jnp.bfloat16)
    grad_in = jnp.dot(normed16.T, d_proj16, preferred_element_type=jnp.float32)
    d_normed = jnp.dot(d_proj16, back_in.T, preferred_element_type=jnp.float32)
    d_base, grad_norm = norm_back(d_normed)
    input_grad = live_cot.astype(jnp.float32) + d_base
    return (activations, input_grad, grad_in, grad_out, grad_norm, grad_gate, grad_conv, grad_head)


def muon_apply(weight, orth, full_shape):
    factor = 0.2 * math.sqrt(max(full_shape[0], full_shape[1]))
    return weight - muon_rate * (factor * orth.astype(jnp.float32) + decay_rate * weight)


MESH = pl.DeviceIdType.MESH
LANES = 128


def places():
    rep = lax.axis_index("rep")
    shard = lax.axis_index("shard")
    core = lax.rem(rep, 2)
    chip = lax.div(rep, 2)
    chips = lax.axis_size("rep") // 2
    shards = lax.axis_size("shard")
    return rep, shard, core, chip, chips, shards


def line_order(shard, shards):
    tables = [
        sorted((z for z in range(shards) if z != here), key=lambda z: (abs(z - here), z))
        for here in range(shards)
    ]
    order = []
    for spot in range(shards - 1):
        value = jnp.int32(tables[0][spot])
        for here in range(1, shards):
            value = jnp.where(shard == here, jnp.int32(tables[here][spot]), value)
        order.append(value)
    return order


def plain_flips(chip, chips):
    count = chips.bit_length() - 1
    return [(1 << j) * (1 - 2 * lax.rem(lax.div(chip, 1 << j), 2)) for j in range(count)]


def core_flips(chip, core, chips):
    base = plain_flips(chip, chips)
    count = len(base)
    return [base[j] + core * (base[count - 1 - j] - base[j]) for j in range(count)]


def block_at(chip, flips, pattern):
    for j, step in enumerate(flips):
        if pattern >> j & 1:
            chip = chip + step
    return chip


def greet_peers(core, chip, shard, chips, shards):
    barrier = pltpu.get_barrier_semaphore()
    peers = [{"rep": 2 * chip + 1 - core}]
    for step in plain_flips(chip, chips):
        peers.append({"rep": 2 * (chip + step) + core})
    for step in range(1, shards):
        peers.append({"shard": lax.rem(shard + step, shards)})
    for peer in peers:
        pl.semaphore_signal(barrier, inc=1, device_id=peer, device_id_type=MESH)
    pl.semaphore_wait(barrier, len(peers))


def remote(src, dst, send, recv, peer):
    return pltpu.make_async_remote_copy(
        src_ref=src, dst_ref=dst, send_sem=send, recv_sem=recv, device_id=peer, device_id_type=MESH
    )


class Spread:
    def __init__(self, slot, sems, index):
        rep, shard, core, chip, chips, shards = places()
        self.slot = slot
        self.xs, self.xr, self.ps, self.pr = [
            (lambda q, s=s: s.at[tuple(index) + (q,)]) for s in sems
        ]
        self.chips, self.chip, self.core = chips, chip, core
        self.flips = core_flips(chip, core, chips)
        self.other_flips = core_flips(chip, 1 - core, chips)
        self.partner = {"rep": 2 * chip + 1 - core}

    def hops(self, pattern):
        ref = self.slot(block_at(self.chip, self.flips, pattern), self.core)
        copies = []
        for phase in range(pattern.bit_length(), len(self.flips)):
            q = pattern + (1 << phase)
            peer = {"rep": 2 * (self.chip + self.flips[phase]) + self.core}
            copies.append(remote(ref, ref, self.xs(q), self.xr(q), peer))
        copies.append(remote(ref, ref, self.ps(pattern), self.pr(pattern), self.partner))
        return copies

    def start(self, pattern):
        for copy in self.hops(pattern):
            copy.start()

    def wait(self, pattern):
        ref = self.slot(block_at(self.chip, self.flips, pattern), self.core)
        phase = pattern.bit_length() - 1
        peer = {"rep": 2 * (self.chip + self.flips[phase]) + self.core}
        remote(ref, ref, self.xs(pattern), self.xr(pattern), peer).wait_recv()

    def wait_partner(self):
        for pattern in range(self.chips):
            ref = self.slot(block_at(self.chip, self.other_flips, pattern), 1 - self.core)
            remote(ref, ref, self.ps(pattern), self.pr(pattern), self.partner).wait_recv()

    def wait_sends(self):
        for pattern in range(self.chips):
            for copy in self.hops(pattern):
                copy.wait_send()


def gather_kernel(in_ref, out_ref, all_in, all_out, send_in, send_out, zs, zr, xs, xr, ps, pr):
    rep, shard, core, chip, chips, shards = places()
    half = jnp.bfloat16
    triples = ((in_ref, send_in, all_in), (out_ref, send_out, all_out))
    for source, send, dst in triples:
        send[...] = source[chip, core].astype(half)
    greet_peers(core, chip, shard, chips, shards)
    order = line_order(shard, shards)
    started = []
    for a, (source, send, dst) in enumerate(triples):
        for other in reversed(order):
            copy = remote(
                send, dst.at[shard, chip, core], zs.at[a, other], zr.at[a, shard], {"shard": other}
            )
            copy.start()
            started.append(copy)
    for source, send, dst in triples:
        dst[shard] = source[...].astype(half)
    spreads = []
    for a, (source, send, dst) in enumerate(triples):
        for spot, other in enumerate(order):

            def slot(block, k, dst=dst, other=other):
                return dst.at[other, block, k]

            here = slot(chip, core)
            remote(here, here, zs.at[a, other], zr.at[a, other], {"shard": other}).wait_recv()
            spreads.append(Spread(slot, (xs, xr, ps, pr), (a, spot)))
            spreads[-1].start(0)
    for spread in spreads:
        for pattern in range(1, chips):
            spread.wait(pattern)
            spread.start(pattern)
    for spread in spreads:
        spread.wait_partner()
    for copy in started:
        copy.wait_send()
    for spread in spreads:
        spread.wait_sends()


def gather_rows(in_weight, out_weight):
    chips = lax.axis_size("rep") // 2
    shards = lax.axis_size("shard")
    half = jnp.bfloat16

    def split(rows):
        return rows.reshape(chips, 2, rows.shape[0] // (2 * chips), rows.shape[1])

    parts = [split(in_weight), split(out_weight)]
    vmem = pl.BlockSpec(memory_space=pltpu.VMEM)
    dma = pltpu.SemaphoreType.DMA
    whole = pl.pallas_call(
        gather_kernel,
        out_shape=[jax.ShapeDtypeStruct((shards,) + p.shape, half) for p in parts],
        in_specs=[vmem, vmem],
        out_specs=[vmem, vmem],
        scratch_shapes=[pltpu.VMEM(p.shape[2:], half) for p in parts]
        + [dma((2, shards))] * 2
        + [dma((2, shards, chips))] * 4,
        compiler_params=pltpu.CompilerParams(
            collective_id=0, has_side_effects=True, vmem_limit_bytes=60 * 1024 * 1024
        ),
    )(*parts)
    return [
        w.reshape(shards * p.shape[0], p.shape[1]) for w, p in zip(whole, (in_weight, out_weight))
    ]


def low_phase(pattern, phases):
    return phases if pattern == 0 else (pattern & -pattern).bit_length() - 1


def update_kernel(names, tail, gin, gout, small, inmom, outmom, *refs):
    k = dict(zip(names, refs))
    rep, shard, core, chip, chips, shards = places()
    f32 = jnp.float32
    half = jnp.bfloat16
    partner = {"rep": 2 * chip + 1 - core}
    flips = core_flips(chip, core, chips)
    other_flips = core_flips(chip, 1 - core, chips)
    base_flips = plain_flips(chip, chips)
    phases = len(flips)
    wide = k["gl"].shape[-1]
    thin = k["gt"].shape[-1]
    count = 4
    kinds = ("l", "l", "t", "o")
    offsets = (0, wide, 2 * wide)
    widths = (wide, wide, thin)
    owners = [number * shards // count for number in range(count)]
    order = (0, 1, 3, 2)
    line = line_order(shard, shards)
    started = []

    def go(copy):
        copy.start()
        started.append(copy)

    def source(number, block, which):
        if number == 3:
            return gout.at[:, :, block, which]
        return gin.at[:, block, which, :, pl.ds(offsets[number], widths[number])]

    local = [
        pltpu.make_async_copy(inmom.at[chip, core], k["momin"], k["lsem"].at[0]),
        pltpu.make_async_copy(outmom.at[:, chip, core], k["momout"], k["lsem"].at[1]),
    ]
    for copy in local:
        copy.start()
    greet_peers(core, chip, shard, chips, shards)
    stages = [
        sorted((d for d in range(1, chips) if low_phase(d, phases) == p), reverse=True)
        for p in range(phases)
    ] + [[0]]
    patterns = [d for stage in stages for d in stage]
    go(remote(small, k["tcore"], k["ts"].at[0], k["tr"].at[0], partner))
    for stage in ([0], range(1, phases + 1)):
        for number in order:
            for p in stage:
                for d in stages[p]:
                    go(
                        remote(
                            source(number, block_at(chip, other_flips, d), 1 - core),
                            k[f"first{number}"].at[d],
                            k["ds"].at[number, d], k["dr"].at[number, d], partner,
                        )
                    )
    for copy in local:
        copy.wait()
    k["momt"][...] = jnp.zeros(k["momt"].shape, f32)
    k["momt"][:, : tail] = k["momin"][:, 2 * wide :]

    def moment(number):
        if number == 3:
            return k["momout"]
        if number == 2:
            return k["momt"]
        return k["momin"].at[:, pl.ds(offsets[number], wide)]

    def send_moment(number):
        return remote(
            moment(number), k["momr" + kinds[number]].at[shard],
            k["ms"].at[number], k["mr"].at[shard], {"shard": owners[number]},
        )

    for number in range(count):

        @pl.when(shard != owners[number])
        def _():
            send_moment(number).start()

        @pl.when(shard == owners[number])
        def _():
            k["momr" + kinds[number]][shard] = moment(number)[...]

    def send_plane(number):
        return remote(
            k[f"sums{number}"].at[0], k["third" + kinds[number]].at[shard],
            k["zs"].at[number], k["zr"].at[shard], {"shard": owners[number]},
        )

    def reduce_step(number, d):
        last = low_phase(d, phases)
        slot = k[f"first{number}"].at[d]
        remote(slot, slot, k["ds"].at[number, d], k["dr"].at[number, d], partner).wait_recv()
        total = source(number, block_at(chip, flips, d), core)[...].astype(f32)
        total = total + slot[...].astype(f32)
        for q in range(last):
            came = d + (1 << q)
            slot = k[f"recv{number}"].at[came]
            peer = {"rep": 2 * (chip + flips[q]) + core}
            remote(slot, slot, k["rs"].at[number, came], k["rr"].at[number, came], peer).wait_recv()
            total = total + slot[...].astype(f32)
        k[f"sums{number}"][d] = total.astype(half)
        if d:
            peer = {"rep": 2 * (chip + flips[last]) + core}
            go(
                remote(
                    k[f"sums{number}"].at[d], k[f"recv{number}"].at[d],
                    k["rs"].at[number, d], k["rr"].at[number, d], peer,
                )
            )
        else:

            @pl.when(shard != owners[number])
            def _():
                send_plane(number).start()

            @pl.when(shard == owners[number])
            def _():
                k["third" + kinds[number]][shard] = k[f"sums{number}"][0]

    def small_step(j):
        if j == 0:
            remote(small, k["tcore"], k["ts"].at[0], k["tr"].at[0], partner).wait_recv()
            k["tacc"][0] = small[...] + k["tcore"][...]
        else:
            slot = k["trecv"].at[j - 1]
            peer = {"rep": 2 * (chip + base_flips[j - 1]) + core}
            remote(slot, slot, k["ts"].at[j], k["tr"].at[j], peer).wait_recv()
            k["tacc"][j] = k["tacc"][j - 1] + slot[...]
        if j < phases:
            peer = {"rep": 2 * (chip + base_flips[j]) + core}
            go(
                remote(
                    k["tacc"].at[j], k["trecv"].at[j], k["ts"].at[j + 1], k["tr"].at[j + 1], peer
                )
            )
        else:
            k["tz"][shard] = k["tacc"][phases]
            for other in line:
                go(
                    remote(
                        k["tacc"].at[phases], k["tz"].at[shard],
                        k["tzs"].at[other], k["tzr"].at[shard], {"shard": other},
                    )
                )

    for number in order:
        for d in stages[0]:
            reduce_step(number, d)
    small_step(0)
    steps = 1
    for turn in range(count + phases - 1):
        for p in range(1, phases + 1):
            spot = turn - (p - 1)
            if 0 <= spot < count:
                for d in stages[p]:
                    reduce_step(order[spot], d)
        if steps <= phases:
            small_step(steps)
            steps += 1

    def grad_slot(number):
        ref = k["g" + kinds[number]]
        if number == 3:
            return lambda block, which: ref.at[:, block, which]
        if number == 2:
            return lambda block, which: ref.at[block, which]
        return lambda block, which: ref.at[number, block, which]

    def orth_slot(number):
        ref = k["o" + kinds[number]]
        if number == 3:
            return lambda block, which: ref.at[:, block, which]
        if number == 2:
            return lambda block, which: ref.at[block, which]
        return lambda block, which: ref.at[number, block, which]

    grad_spreads = [
        Spread(grad_slot(number), [k["g" + s] for s in ("xs", "xr", "ps", "pr")], (number,))
        for number in range(count)
    ]
    orth_spreads = [
        Spread(orth_slot(number), [k["o" + s] for s in ("xs", "xr", "ps", "pr")], (number,))
        for number in range(count)
    ]

    def grads_first():
        for number in order:

            @pl.when(shard != owners[number])
            def _():
                slot = grad_slot(number)(chip, core)
                remote(
                    slot, slot, k["gzs"].at[0], k["gzr"].at[number], {"shard": owners[number]}
                ).wait_recv()

            grad_spreads[number].start(0)

    def grads_second():
        for pattern in range(1, chips):
            for number in order:
                grad_spreads[number].wait(pattern)
                grad_spreads[number].start(pattern)

    def hooks(turn):
        pl.when(turn == 1)(grads_first)
        pl.when(turn == 3)(grads_second)

    def finish_poly(gram, gram_ref, poly_ref):
        gram_ref[...] = gram.astype(half)
        gram = gram_ref[...]
        square = jnp.dot(gram, gram, preferred_element_type=f32)
        poly_ref[...] = (
            schulz_coeffs[1] * gram.astype(f32) + schulz_coeffs[2] * square
        ).astype(half)

    def iterate_left(cur, gram_ref, poly_ref):
        tall, across = cur.shape
        size = min(tall, across)

        @pl.loop(0, NS_STEPS)
        def _(turn):
            hooks(turn)
            now = cur[...]
            finish_poly(
                lax.dot_general(now, now, (((1,), (1,)), ((), ())), preferred_element_type=f32),
                gram_ref, poly_ref,
            )
            for q in range(across // size):
                part = cur[:, q * size : (q + 1) * size]
                cur[:, q * size : (q + 1) * size] = (
                    schulz_coeffs[0] * part.astype(f32)
                    + jnp.dot(poly_ref[...], part, preferred_element_type=f32)
                ).astype(half)

    def iterate_right(cur, gram_ref, poly_ref):
        tall, across = cur.shape
        size = math.gcd(tall, 512)

        @pl.loop(0, NS_STEPS)
        def _(turn):
            hooks(turn)
            gram = jnp.zeros((across, across), f32)
            for q in range(tall // size):
                part = cur[q * size : (q + 1) * size]
                gram = gram + lax.dot_general(
                    part, part, (((0,), (0,)), ((), ())), preferred_element_type=f32
                )
            finish_poly(gram, gram_ref, poly_ref)
            for q in range(tall // size):
                part = cur[q * size : (q + 1) * size]
                cur[q * size : (q + 1) * size] = (
                    schulz_coeffs[0] * part.astype(f32)
                    + jnp.dot(part, poly_ref[...], preferred_element_type=f32)
                ).astype(half)

    def own_work(kind, number):
        third, momr, buf, cur = [k[name + kind] for name in ("third", "momr", "buf", "cur")]
        gsend = k["gsend" + kind]
        folded = kind == "o"

        def piece(block, which):
            return buf.at[:, :, block, which] if folded else buf.at[:, block, which]

        def rows(ref, block, which):
            if kind == "l":
                return ref.at[number, block, which]
            return ref.at[:, block, which] if folded else ref.at[block, which]

        for other in line:
            slot = third.at[other]
            remote(slot, slot, k["zs"].at[0], k["zr"].at[other], {"shard": other}).wait_recv()
            slot = momr.at[other]
            remote(slot, slot, k["ms"].at[0], k["mr"].at[other], {"shard": other}).wait_recv()
        total = third[0].astype(f32)
        for z in range(1, shards):
            total = total + third[z].astype(f32)
        merged = (momentum_keep * momr[...] + total).astype(half)
        if folded:
            buf[:, :, chip, core] = merged
        else:
            buf[:, chip, core] = merged
        spread = Spread(piece, [k["b" + s] for s in ("xs", "xr", "ps", "pr")], ())
        spread.start(0)
        gsend[...] = total.astype(half)

        def send_grad(other):
            return remote(
                gsend.at[other], rows(k["g" + kind], chip, core),
                k["gzs"].at[other], k["gzr"].at[number], {"shard": other},
            )

        for other in line:
            send_grad(other).start()
        rows(k["g" + kind], chip, core)[...] = gsend[shard]
        for pattern in range(1, chips):
            spread.wait(pattern)
            spread.start(pattern)
        spread.wait_partner()
        matrix = buf[...].reshape(cur.shape).astype(f32)
        frobenius = jnp.sqrt(jnp.sum(matrix * matrix))
        cur[...] = (matrix / (frobenius + 1e-07)).astype(half)
        if kind == "l":
            iterate_left(cur, k["graml"], k["polyl"])
        else:
            iterate_right(cur, k["gram" + kind], k["poly" + kind])
        spread.wait_sends()
        buf[...] = cur[...].reshape(buf.shape)

        def back(other):
            part = buf.at[other]
            part = part.at[:, chip, core] if folded else part.at[chip, core]
            return remote(
                part, rows(k["o" + kind], chip, core),
                k["ozs"].at[other], k["ozr"].at[number], {"shard": other},
            )

        for other in line:
            back(other).start()
        if kind == "l":
            k["ol"][number] = buf[shard]
        else:
            k["o" + kind][...] = buf[shard]
        for other in line:
            send_grad(other).wait_send()
            back(other).wait_send()

    def is_owner(numbers):
        flag = shard == owners[numbers[0]]
        for number in numbers[1:]:
            flag = jnp.logical_or(flag, shard == owners[number])
        return flag

    pl.when(is_owner((0, 1)))(lambda: own_work("l", lax.div(shard * count, shards)))
    pl.when(is_owner((2,)))(lambda: own_work("t", 2))
    pl.when(is_owner((3,)))(lambda: own_work("o", 3))
    if shards > count:

        @pl.when(jnp.logical_not(is_owner(range(count))))
        def _():
            grads_first()
            grads_second()

    back_order = (2, 0, 1, 3)
    for number in back_order:

        @pl.when(shard != owners[number])
        def _():
            slot = orth_slot(number)(chip, core)
            remote(
                slot, slot, k["ozs"].at[0], k["ozr"].at[number], {"shard": owners[number]}
            ).wait_recv()
            orth_spreads[number].start(0)

    for other in line:
        slot = k["tz"].at[other]
        remote(slot, slot, k["tzs"].at[other], k["tzr"].at[other], {"shard": other}).wait_recv()
    total = k["tz"][0]
    for z in range(1, shards):
        total = total + k["tz"][z]
    k["ftiny"][...] = total
    for spread in grad_spreads:
        spread.wait_partner()
    for number in back_order:

        @pl.when(shard != owners[number])
        def _():
            for pattern in range(1, chips):
                orth_spreads[number].wait(pattern)
                orth_spreads[number].start(pattern)

    for copy in started:
        copy.wait_send()
    for number in range(count):

        @pl.when(shard != owners[number])
        def _():
            send_moment(number).wait_send()
            send_plane(number).wait_send()

        grad_spreads[number].wait_sends()
    for number in back_order:

        @pl.when(shard != owners[number])
        def _():
            orth_spreads[number].wait_partner()
            orth_spreads[number].wait_sends()


def reduce_and_orthogonalize(grad_in, grad_out, small, in_moment, out_moment, wide):
    chips = lax.axis_size("rep") // 2
    shards = lax.axis_size("shard")
    half = jnp.bfloat16
    f32 = jnp.float32
    height, columns = grad_in.shape
    depth = grad_out.shape[1]
    rows = height // (shards * chips * 2)
    folds = grad_out.shape[0] // height
    tail = columns - 2 * wide
    thin = -(-tail // LANES) * LANES
    gin = jnp.pad(grad_in, ((0, 0), (0, thin - tail))).reshape(
        shards, chips, 2, rows, 2 * wide + thin
    )
    gout = grad_out.reshape(shards, folds, chips, 2, rows, depth)
    inmom = in_moment.reshape(chips, 2, rows, columns)
    outmom = out_moment.reshape(folds, chips, 2, rows, depth)
    outs = {
        "gl": ((2, chips, 2, rows, wide), half),
        "gt": ((chips, 2, rows, thin), half),
        "go": ((folds, chips, 2, rows, depth), half),
        "ol": ((2, chips, 2, rows, wide), half),
        "ot": ((chips, 2, rows, thin), half),
        "oo": ((folds, chips, 2, rows, depth), half),
        "ftiny": (small.shape, f32),
    }
    tails = [(rows, wide), (rows, wide), (rows, thin), (folds, rows, depth)]
    scratch = {
        "momin": ((rows, columns), f32),
        "momout": ((folds, rows, depth), f32),
        "momt": ((rows, thin), f32),
        "tcore": (small.shape, f32),
        "tacc": ((chips.bit_length(),) + small.shape, f32),
        "trecv": ((chips.bit_length(),) + small.shape, f32),
        "tz": ((shards,) + small.shape, f32),
    }
    for number, part in enumerate(tails):
        for name in ("first", "sums", "recv"):
            scratch[f"{name}{number}"] = ((chips, shards) + part, half)
    full = {
        "l": ((shards, chips, 2, rows, wide), (height, wide), height),
        "t": ((shards, chips, 2, rows, thin), (height, thin), thin),
        "o": ((shards, folds, chips, 2, rows, depth), (height * folds, depth), depth),
    }
    for kind, number in (("l", 0), ("t", 2), ("o", 3)):
        scratch["third" + kind] = ((shards, shards) + tails[number], half)
        scratch["momr" + kind] = ((shards,) + tails[number], f32)
        scratch["gsend" + kind] = ((shards,) + tails[number], half)
        scratch["buf" + kind] = (full[kind][0], half)
        scratch["cur" + kind] = (full[kind][1], half)
        scratch["gram" + kind] = ((full[kind][2],) * 2, half)
        scratch["poly" + kind] = ((full[kind][2],) * 2, half)
    sems = {
        "lsem": (2,),
        "ts": (chips.bit_length(),),
        "tr": (chips.bit_length(),),
        "tzs": (shards,),
        "tzr": (shards,),
        "zs": (4,),
        "zr": (shards,),
        "ms": (4,),
        "mr": (shards,),
        "gzs": (shards,),
        "gzr": (4,),
        "ozs": (shards,),
        "ozr": (4,),
    }
    for name in ("ds", "dr", "rs", "rr"):
        sems[name] = (4, chips)
    for name in ("xs", "xr", "ps", "pr"):
        sems["b" + name] = (chips,)
        sems["g" + name] = (4, chips)
        sems["o" + name] = (4, chips)
    vmem = pl.BlockSpec(memory_space=pltpu.VMEM)
    anywhere = pl.BlockSpec(memory_space=pl.ANY)
    names = list(outs) + list(scratch) + list(sems)
    return pl.pallas_call(
        functools.partial(update_kernel, names, tail),
        out_shape=[jax.ShapeDtypeStruct(s, d) for s, d in outs.values()],
        in_specs=[vmem] * 3 + [anywhere] * 2,
        out_specs=[vmem] * len(outs),
        scratch_shapes=[pltpu.VMEM(s, d) for s, d in scratch.values()]
        + [pltpu.SemaphoreType.DMA(s) for s in sems.values()],
        compiler_params=pltpu.CompilerParams(
            collective_id=1, has_side_effects=True, vmem_limit_bytes=60 * 1024 * 1024
        ),
    )(gin, gout, small, inmom, outmom)


def finish_kernel(
    sizes, gl, gt, go, ol, ot, oo, tiny, in_w, out_w, in_m, out_m,
    p_norm, p_gate, p_conv, p_head, a_norm, a_gate, a_conv, a_head,
    grad_in, grad_out, grad_norm, grad_gate, grad_conv, grad_head,
    new_in, new_out, mom_in, mom_out,
    n_norm, n_gate, n_conv, n_head, s_norm, s_gate, s_conv, s_head,
):
    f32 = jnp.float32
    wide = gl.shape[-1]
    tail = in_w.shape[1] - 2 * wide
    spans = ((0, wide), (wide, wide), (2 * wide, tail))
    for number, (low, width) in enumerate(spans):
        if number < 2:
            grad, orth = gl[number].astype(f32), ol[number].astype(f32)
        else:
            grad, orth = gt[:, :width].astype(f32), ot[:, :width].astype(f32)
        here = slice(low, low + width)
        grad_in[:, here] = grad
        mom_in[:, here] = momentum_keep * in_m[:, here] + grad
        new_in[:, here] = muon_apply(in_w[:, here], orth, sizes[number])
    grad = go[...].astype(f32)
    grad_out[...] = grad
    mom_out[...] = momentum_keep * out_m[...] + grad
    new_out[...] = muon_apply(out_w[...], oo[...].astype(f32), sizes[3])

    def adam(grad, param, state):
        first = beta_first * state[0] + (1.0 - beta_first) * grad
        second = beta_second * state[1] + (1.0 - beta_second) * grad * grad
        first_hat = first / (1.0 - beta_first**ADAM_STEP)
        second_hat = second / (1.0 - beta_second**ADAM_STEP)
        updated = param - adam_rate * (
            first_hat / (jnp.sqrt(second_hat) + adam_eps) + decay_rate * param
        )
        return updated, first, second

    taps = p_conv.shape[0]
    conv = tiny[:taps]
    grad_conv[...] = conv
    n_conv[...], s_conv[0], s_conv[1] = adam(conv, p_conv[...], (a_conv[0], a_conv[1]))
    for row, grad_ref, p, a, n, s in (
        (taps, grad_gate, p_gate, a_gate, n_gate, s_gate),
        (taps + 1, grad_norm, p_norm, a_norm, n_norm, s_norm),
    ):
        grad = tiny[row : row + 1, : p.shape[1]]
        grad_ref[...] = grad
        n[...], s[0:1], s[1:2] = adam(grad, p[...], (a[0:1], a[1:2]))
    heads = p_head.shape[1]
    for i in range(p_head.shape[0]):
        grad = tiny[taps + 2 : taps + 3, i * LANES : i * LANES + heads]
        one = slice(i, i + 1)
        grad_head[one] = grad
        n_head[one], s_head[0, one], s_head[1, one] = adam(
            grad, p_head[one], (a_head[0, one], a_head[1, one])
        )


def pack_small(grad_norm, grad_gate, grad_conv, grad_head):
    width = grad_conv.shape[1]

    def fit(row):
        return jnp.pad(row, ((0, 0), (0, width - row.shape[1])))

    heads = [jnp.pad(grad_head[i][None], ((0, 0), (0, LANES - grad_head.shape[1]))) for i in range(3)]
    packed = jnp.concatenate(
        [grad_conv, fit(grad_gate[None]), fit(grad_norm[None]), fit(jnp.concatenate(heads, 1))], 0
    )
    return jnp.pad(packed, ((0, -packed.shape[0] % 8), (0, 0)))


def local(
    tokens,
    cotangent,
    block_fill,
    block_start,
    in_weight,
    out_weight,
    in_moment,
    out_moment,
    norm_gain,
    gate_gain,
    conv_params,
    head_params,
    adam_norm,
    adam_gate,
    adam_conv,
    adam_head,
):
    shards = lax.axis_size("shard")
    replicas = lax.axis_size("rep")
    whole_in, whole_out = gather_rows(in_weight, out_weight)
    results = device_pass(
        tokens,
        cotangent,
        block_fill,
        block_start,
        whole_in,
        whole_out,
        whole_in,
        whole_out,
        norm_gain,
        gate_gain,
        conv_params,
        head_params,
    )
    activations, input_grad, grad_in, grad_out, grad_norm, grad_gate, grad_conv, grad_head = results
    scale = 1.0 / math.sqrt(tokens.shape[0] * shards * replicas)
    wide = gate_gain.shape[0]
    gl, gt, go, ol, ot, oo, tiny = reduce_and_orthogonalize(
        (scale * grad_in).astype(jnp.bfloat16),
        (scale * grad_out).astype(jnp.bfloat16),
        scale * pack_small(grad_norm, grad_gate, grad_conv, grad_head),
        in_moment,
        out_moment,
        wide,
    )
    rows = in_weight.shape[0]
    tail = in_weight.shape[1] - 2 * wide
    sizes = (
        (rows * shards, wide),
        (rows * shards, wide),
        (rows * shards, tail),
        (out_weight.shape[0] * shards, out_weight.shape[1]),
    )
    pieces = []
    for l, t, o in ((gl, gt, go), (ol, ot, oo)):
        pieces += [l.reshape(2, rows, wide), t.reshape(rows, -1), o.reshape(out_weight.shape)]
    params = [norm_gain[None], gate_gain[None], conv_params, head_params]
    states = [adam_norm, adam_gate, adam_conv, adam_head]
    like = [in_weight, out_weight] + params + [in_weight, out_weight] * 2 + params + states
    vmem = pl.BlockSpec(memory_space=pltpu.VMEM)
    done = pl.pallas_call(
        functools.partial(finish_kernel, sizes),
        out_shape=[jax.ShapeDtypeStruct(a.shape, a.dtype) for a in like],
        in_specs=[vmem] * (11 + 8),
        out_specs=[vmem] * len(like),
        compiler_params=pltpu.CompilerParams(vmem_limit_bytes=60 * 1024 * 1024),
    )(*pieces, tiny, in_weight, out_weight, in_moment, out_moment, *params, *states)
    done = list(done)
    for spot, gain in ((2, norm_gain), (3, gate_gain), (10, norm_gain), (11, gate_gain)):
        done[spot] = done[spot].reshape(gain.shape)
    return (activations, input_grad, *done)


def solution(mesh):
    return jax.shard_map(
        local,
        mesh=mesh,
        in_specs=(
            P(("rep", "shard"), None),
            P(("rep", "shard"), None),
            P(("rep", "shard")),
            P(("rep", "shard")),
            P("shard", None),
            P("shard", None),
            P("shard", None),
            P("shard", None),
            P(),
            P(),
            P(),
            P(),
            P(),
            P(),
            P(),
            P(),
        ),
        out_specs=(
            P(("rep", "shard"), None),
            P(("rep", "shard"), None),
            P("shard", None),
            P("shard", None),
            P(),
            P(),
            P(),
            P(),
            P("shard", None),
            P("shard", None),
            P("shard", None),
            P("shard", None),
            P(),
            P(),
            P(),
            P(),
            P(),
            P(),
            P(),
            P(),
        ),
        check_vma=False,
    )
```

time: 176 us -> 177 us (level)
  other arithmetic: 26.4 us -> 11.1 us
  local copies, waits for them, and re-layouts: 11.6 us -> 21.2 us
  Pallas kernels: 115 us -> 124 us
    unnamed x73 -> x48, local copies, waits for them, and re-layouts: 5.21 us -> 17.2 us
    pallas_call x1, Pallas kernels: 32.8 us -> 41 us  [gather_rows(): pl.pallas_call(gather_kernel, out_shape=[jax.ShapeDtypeStruct((shards,) +...]
    another operation x10 -> x1, other arithmetic: 8.15 us -> 0.18 us
    convert_element_type x2 -> x0, local copies, waits for them, and re-layouts: 3.8 us -> none  [the longest x1 2.73 us: local(): (scale * grad_in).astype(jnp.bfloat16)]
    pad x1, local copies, waits for them, and re-layouts: 0.02 us -> 3.37 us  [reduce_and_orthogonalize(): jnp.pad(grad_in, ((0, 0), (0, thin - tail)))]
    convert_element_type x3 -> x0, other arithmetic: 2.25 us -> none  [the longest x1 1.39 us: local(): in_half = in_weight.astype(jnp.bfloat16)]
    sub x5 -> x0, other arithmetic: 2.1 us -> none  [the longest x3 1.89 us: adam_apply(): param - adam_rate * (first_hat / (jnp.sqrt(second_hat) + adam_eps) + deca...]
where the time goes in v1:
time: 177 us
  Pallas kernels  124 us (70%)
  local copies, waits for them, and re-layouts  21.2 us (12%)
  matrix products  19.6 us (11%)
  other arithmetic  11.1 us (6%)
    pallas_call x1, Pallas kernels, reduce_and_orthogonalize(): pl.pallas_call(functools.partial(update_kernel, names, tail), out_shape=[...  77.7 us
    pallas_call x1, Pallas kernels, gather_rows(): pl.pallas_call(gather_kernel, out_shape=[jax.ShapeDtypeStruct((shards,) +...  41 us
    unnamed x48, local copies, waits for them, and re-layouts  17.2 us
    dot_general x3, matrix products, mixer(): jnp.einsum('hts,shp->thp', decay * scores[None], weighted, precision=ssd_...  9.94 us
    pallas_call x1, Pallas kernels, local(): pl.pallas_call(functools.partial(finish_kernel, sizes), out_shape=[jax.Sh...  5.1 us

profile of v1, /device:TPU:0, one launch (start us, length us, event | category | flops | bytes accessed | tf_op | source)
XLA Modules:
  0.0 176.6 jit_solution(5697711185198161768)
XLA Ops:
  0.7 2.7 %copy.50.in_w = f32[128,2320]{1,0:T(8,128)} copy(f32[128,2320]{0,1:T(8,128)} %param.20) | data formatting | bytes 2375680 | tf_op args[4]
  3.4 41.0 %shard_map.311 = (bf16[4,4,2,16,2320]{4,3,2,1,0:T(8,128)(2,1)}, bf16[4,4,2,32,512]{4,3,2,1,0:T(8,128)(2,1)}) custom-call(f32[4,2,16,2320]{3,2,1,0:T(8,128)} %bitcast.70, f32[4,2,32,512]{3,2,1,0:T(8,128)} %bitcast.76), custom_call_target="tpu_custom_call" | custom-call | tf_op jit(solution)/shard_map/pallas_call | solution.py:281
  44.5 0.1 fusion.44
  44.7 2.8 %fusion.60 = f32[256,2320]{0,1:T(8,128)S(1)} fusion(bf16[512,2320]{1,0:T(8,128)(2,1)} %bitcast.74, bf16[256,512]{1,0:T(8,128)(2,1)S(1)} %copy-done.3, f32[512]{0:T(512)S(1)} %copy-done.13, f32[256]{0:T(256)S(1)} %fusion.75), kind=kOutput, calls=%fused_computation.91 | convolution fusion | flops 608698368 | bytes 5016576 | tf_op jit(solution)/shard_map/dot_general | solution.py:96
  47.5 0.2 reduce-window.9
  47.9 0.7 copy-done.9
  48.9 2.5 %fusion.30 = (f32[256,1280]{0,1:T(8,128)S(1)}, f32[256,1280]{0,1:T(8,128)S(1)}) fusion(f32[256]{0:T(256)S(1)} %get-tuple-element.157, f32[253,1280]{0,1:T(8,128)S(1)} %slice.98, f32[1280]{0:T(1024)S(1)} %get-tuple-element.127, f32[256]{0:T(256)S(1)} %get-tuple-element.158, f32[254,1280]{0,1:T(8,128)S(1)} %slice.97, f32[1280]{0:T(1024)S(1)} %get-tuple-element.124, ...), kind=kLoop, calls=%fused_computation.40 | loop fusion | flops 4915200 | bytes 7862272 | tf_op jit(solution)/shard_map/jvp(jit(silu))/mul | solution.py:52
  51.4 0.3 fusion.54
  51.7 0.1 compare_select_fusion.2
  51.8 0.2 fusion.50
  52.0 0.2 fusion.51
  52.2 2.8 %fusion.25 = f32[256,16,64]{0,2,1:T(8,128)S(1)} fusion(f32[256,256]{1,0:T(8,128)S(1)} %fusion.54, f32[16,256]{1,0:T(8,128)S(1)} %fusion.50, pred[256,256]{1,0:T(8,128)(4,1)S(1)} %fusion.51, f32[256,16,64]{0,2,1:T(8,128)S(1)} %bitcast.83, f32[16]{0:T(128)S(1)} %get-tuple-element.153, f32[256,16]{0,1:T(8,128)S(1)} %compare_select_fusion.2), kind=kOutput, calls=%fused_computation.28 | convolution fusion | flops 407633920 | bytes 2457664 | tf_op jit(solution)/shard_map/jvp(hts,shp->thp)/dot_general | solution.py:67
  55.0 0.4 multiply_reduce_fusion.9
  55.4 0.5 copy-done.4
  56.0 0.4 copy-done.8
  56.3 1.5 fusion.32
  57.8 0.6 multiply_reduce_fusion.6
  58.5 1.0 multiply_reduce_fusion.5
  59.4 2.3 %multiply_reduce_fusion.7 = (f32[256,16]{0,1:T(8,128)S(1)}, f32[256,16,64]{0,2,1:T(8,128)S(1)}) fusion(f32[256,1280]{0,1:T(8,128)S(1)} %get-tuple-element.141, f32[256,16]{0,1:T(8,128)S(1)} %compare_select_fusion.2, f32[256,16,64]{0,2,1:T(8,128)S(1)} %bitcast.80, f32[16]{0:T(128)S(1)} %get-tuple-element.153, f32[16,64,256]{2,1,0:T(8,128)S(1)} %bitcast.81, ...), kind=kOutput, calls=%fused_computation.52 | convolution fusion | flops 408154112 | bytes 4588032 | tf_op jit(solution)/shard_map/transpose(jvp(hts,shp->thp))/dot_general | solution.py:67
  61.8 4.9 %fusion.8 = (f32[16,256]{1,0:T(8,128)S(1)}, f32[16,256]{1,0:T(8,128)S(1)}, f32[256,256]{1,0:T(8,128)S(1)}) fusion(f32[256,256]{1,0:T(8,128)S(1)} %fusion.54, f32[16,256]{1,0:T(8,128)S(1)} %fusion.50, pred[256,256]{1,0:T(8,128)(4,1)S(1)} %fusion.51, f32[16,64,256]{2,1,0:T(8,128)S(1)} %bitcast.82, f32[256,16,64]{0,2,1:T(8,128)S(1)} %bitcast.84, ...), kind=kOutput, calls=%fused_computation.10 | convolution fusion | flops 414375936 | bytes 2752512 | tf_op jit(solution)/shard_map/transpose(jvp(hts,shp->thp))/dot_general | solution.py:67
  66.6 0.2 fusion.56
  66.9 0.3 fusion.52
  67.2 0.8 multiply_reduce_fusion.4
  68.0 1.3 multiply_reduce_fusion.3
  69.3 0.6 slice_multiply_fusion
  69.9 0.6 slice_multiply_fusion.1
  70.5 0.6 slice_multiply_fusion.2
  71.1 0.8 multiply_reduce_fusion.1
  71.8 0.3 fusion.83
  72.1 0.6 copy-done
  72.8 1.0 fusion.42
  73.8 1.0 fusion.43
  74.9 0.9 fusion
  75.7 2.7 %copy.65 = bf16[512,2320]{1,0:T(8,128)(2,1)} copy(bf16[512,2320]{0,1:T(8,128)(2,1)S(1)} %fusion) | data formatting | bytes 4751360
  78.5 3.4 %pad.91.clone = bf16[512,2432]{1,0:T(8,128)(2,1)} pad(bf16[512,2320]{1,0:T(8,128)(2,1)} %copy.65, bf16[]{:T(256)} %constant.64.clone.1), padding=0_0x0_112 | pad | bytes 4866050 | tf_op jit(solution)/shard_map/jit(_pad)/pad | solution.py:701
  81.8 1.5 multiply_convert_fusion
  83.4 0.1 reduce_sum.198
  83.7 0.6 fusion.62.small
  84.3 1.5 copy.54.in_m
  85.8 77.7 %shard_map.312 = (bf16[2,4,2,16,1024]{4,3,2,1,0:T(8,128)(2,1)}, bf16[4,2,16,384]{3,2,1,0:T(8,128)(2,1)}, bf16[2,4,2,16,512]{4,3,2,1,0:T(8,128)(2,1)}, bf16[2,4,2...) custom-call(bf16[4,4,2,16,2432]{4,3,2,1,0:T(8,128)(2,1)} %bitcast.72, ...), custom_call_target="tpu_custom_call" | custom-call | tf_op jit(solution)/shard_map/pallas_call | solution.py:766
  163.5 0.6 copy.57.a_conv
  164.1 0.6 copy.58.a_head
  164.7 5.1 %shard_map.313 = (f32[128,2320]{1,0:T(8,128)}, f32[256,512]{1,0:T(8,128)}, f32[1,512]{1,0:T(1,128)}, f32[1,1024]{1,0:T(1,128)}, f32[5,1280]{1,0:T(8,128)}, /*ind...) custom-call(bf16[2,128,1024]{2,1,0:T(8,128)(2,1)} %bitcast.86, ...), custom_call_target="tpu_custom_call" | custom-call | tf_op jit(solution)/shard_map/pallas_call | solution.py:909
  169.8 2.8 %copy.59 = f32[128,2320]{0,1:T(8,128)} copy(f32[128,2320]{1,0:T(8,128)} %get-tuple-element.96) | data formatting | bytes 2375680
  172.6 1.4 copy.60
  174.0 1.4 copy.61
  175.4 0.6 copy.62
  176.1 0.6 copy.63
  (58 shorter events, 0.9 us)
Async XLA Ops:
  3.4 41.0 %copy-start.17 = (s32[2]{0:T(128)S(1)}, s32[2]{0:T(128)}, u32[]{:S(2)}) copy-start(s32[2]{0:T(128)} %param.18) | copy-start | bytes 28
  3.4 41.1 %copy-start.3 = (bf16[256,512]{1,0:T(8,128)(2,1)S(1)}, bf16[256,512]{1,0:T(8,128)(2,1)}, u32[]{:S(2)}) copy-start(bf16[256,512]{1,0:T(8,128)(2,1)} %param.16) | copy-start | bytes 786436
  3.4 41.2 %copy-start.13 = (f32[512]{0:T(512)S(1)}, f32[512]{0:T(512)}, u32[]{:S(2)}) copy-start(f32[512]{0:T(512)} %param.24) | copy-start | bytes 6148
  44.6 2.9 %copy-start.18 = (s32[2]{0:T(128)S(1)}, s32[2]{0:T(128)}, u32[]{:S(2)}) copy-start(s32[2]{0:T(128)} %param.19) | copy-start | bytes 28
  47.8 0.8 copy-start.9
  48.9 2.8 %copy-start.14 = (f32[3,16]{1,0:T(4,128)S(1)}, f32[3,16]{1,0:T(4,128)}, u32[]{:S(2)}) copy-start(f32[3,16]{1,0:T(4,128)} %p_head.1) | copy-start | bytes 580
  55.0 1.0 copy-start.4
  55.0 1.3 copy-start.8
  55.0 1.3 copy-start.11
  56.3 1.5 copy-start.1
  71.1 1.7 copy-start
  78.5 3.4 %copy-start.2 = (bf16[256,512]{1,0:T(8,128)(2,1)S(1)}, bf16[256,512]{1,0:T(8,128)(2,1)}, u32[]{:S(2)}) copy-start(bf16[256,512]{1,0:T(8,128)(2,1)} %param.17) | copy-start | bytes 786436
  81.8 2.5 %copy-start.7 = (f32[128,2320]{0,1:T(8,128)S(1)}, f32[128,2320]{0,1:T(8,128)}, u32[]{:S(2)}) copy-start(f32[128,2320]{0,1:T(8,128)} %param.22) | copy-start | bytes 3563524
  85.8 77.7 %copy-start.12 = (f32[2,5,1280]{2,0,1:T(2,128)S(1)}, f32[2,5,1280]{2,0,1:T(2,128)}, u32[]{:S(2)}) copy-start(f32[2,5,1280]{2,0,1:T(2,128)} %param.30) | copy-start | bytes 153604
  85.8 78.3 %copy-start.16 = (f32[2,3,16]{2,0,1:T(2,128)S(1)}, f32[2,3,16]{2,0,1:T(2,128)}, u32[]{:S(2)}) copy-start(f32[2,3,16]{2,0,1:T(2,128)} %param.31) | copy-start | bytes 1156
  169.8 2.8 %copy-start.6 = (f32[128,2320]{1,0:T(8,128)S(1)}, f32[128,2320]{1,0:T(8,128)}, u32[]{:S(2)}) copy-start(f32[128,2320]{1,0:T(8,128)} %get-tuple-element.102) | copy-start | bytes 3563524
  172.6 1.4 copy-start.5
  174.0 1.4 copy-start.10
  174.0 2.0 %copy-start.15 = (f32[2,3,16]{2,1,0:T(4,128)S(1)}, f32[2,3,16]{2,1,0:T(4,128)}, u32[]{:S(2)}) copy-start(f32[2,3,16]{2,1,0:T(4,128)} %get-tuple-element.113) | copy-start | bytes 1156

commit v2 on v1

--- a/solution.py
+++ b/solution.py
@@ -104,14 +104,13 @@
     activations = jnp.where(live[:, None], base + branch, 0.0).astype(jnp.bfloat16)
     live_cot = jnp.where(live[:, None], cotangent, jnp.zeros_like(cotangent))
     d_mixed = jnp.dot(live_cot, back_out.T, preferred_element_type=jnp.float32)
-    grad_out = jnp.dot(mixed16.T, live_cot, preferred_element_type=jnp.float32)
     d_proj, grad_conv, grad_head, grad_gate = mixer_back(d_mixed)
     d_proj16 = d_proj.astype(jnp.bfloat16)
-    grad_in = jnp.dot(normed16.T, d_proj16, preferred_element_type=jnp.float32)
     d_normed = jnp.dot(d_proj16, back_in.T, preferred_element_type=jnp.float32)
     d_base, grad_norm = norm_back(d_normed)
     input_grad = live_cot.astype(jnp.float32) + d_base
-    return (activations, input_grad, grad_in, grad_out, grad_norm, grad_gate, grad_conv, grad_head)
+    factors = (normed16, d_proj16, mixed16, live_cot)
+    return (activations, input_grad, factors, grad_norm, grad_gate, grad_conv, grad_head)
 
 
 def muon_apply(weight, orth, full_shape):
@@ -152,10 +151,9 @@
     return [(1 << j) * (1 - 2 * lax.rem(lax.div(chip, 1 << j), 2)) for j in range(count)]
 
 
-def core_flips(chip, core, chips):
-    base = plain_flips(chip, chips)
-    count = len(base)
-    return [base[j] + core * (base[count - 1 - j] - base[j]) for j in range(count)]
+def turned_flips(chip, chips, turned):
+    flips = plain_flips(chip, chips)
+    return flips[::-1] if turned else flips
 
 
 def block_at(chip, flips, pattern):
@@ -184,15 +182,14 @@
 
 
 class Spread:
-    def __init__(self, slot, sems, index):
+    def __init__(self, slot, sems, index, turned):
         rep, shard, core, chip, chips, shards = places()
         self.slot = slot
         self.xs, self.xr, self.ps, self.pr = [
             (lambda q, s=s: s.at[tuple(index) + (q,)]) for s in sems
         ]
         self.chips, self.chip, self.core = chips, chip, core
-        self.flips = core_flips(chip, core, chips)
-        self.other_flips = core_flips(chip, 1 - core, chips)
+        self.flips = turned_flips(chip, chips, turned)
         self.partner = {"rep": 2 * chip + 1 - core}
 
     def hops(self, pattern):
@@ -217,7 +214,7 @@
 
     def wait_partner(self):
         for pattern in range(self.chips):
-            ref = self.slot(block_at(self.chip, self.other_flips, pattern), 1 - self.core)
+            ref = self.slot(block_at(self.chip, self.flips, pattern), 1 - self.core)
             remote(ref, ref, self.ps(pattern), self.pr(pattern), self.partner).wait_recv()
 
     def wait_sends(self):
@@ -226,89 +223,159 @@
                 copy.wait_send()
 
 
-def gather_kernel(in_ref, out_ref, all_in, all_out, send_in, send_out, zs, zr, xs, xr, ps, pr):
+def gather_kernel(
+    in_ref, out_ref, mom_ref, all_in, all_out, mom_rows,
+    flat_in, send_in, send_out, zs, zr, xs, xr, ps, pr,
+):
     rep, shard, core, chip, chips, shards = places()
     half = jnp.bfloat16
-    triples = ((in_ref, send_in, all_in), (out_ref, send_out, all_out))
-    for source, send, dst in triples:
-        send[...] = source[chip, core].astype(half)
+    rows = flat_in.shape[1]
+    turned = in_ref[...].T
+    for j in range(2 * chips):
+        flat_in[j] = turned[j * rows : (j + 1) * rows]
+    send_in[...] = flat_in[2 * chip + core].astype(half)
+    send_out[...] = out_ref[chip, core].astype(half)
     greet_peers(core, chip, shard, chips, shards)
-    order = line_order(shard, shards)
-    started = []
-    for a, (source, send, dst) in enumerate(triples):
-        for other in reversed(order):
-            copy = remote(
-                send, dst.at[shard, chip, core], zs.at[a, other], zr.at[a, shard], {"shard": other}
-            )
-            copy.start()
-            started.append(copy)
-    for source, send, dst in triples:
-        dst[shard] = source[...].astype(half)
-    spreads = []
-    for a, (source, send, dst) in enumerate(triples):
-        for spot, other in enumerate(order):
-
-            def slot(block, k, dst=dst, other=other):
-                return dst.at[other, block, k]
-
-            here = slot(chip, core)
-            remote(here, here, zs.at[a, other], zr.at[a, other], {"shard": other}).wait_recv()
-            spreads.append(Spread(slot, (xs, xr, ps, pr), (a, spot)))
-            spreads[-1].start(0)
-    for spread in spreads:
-        for pattern in range(1, chips):
-            spread.wait(pattern)
-            spread.start(pattern)
-    for spread in spreads:
-        spread.wait_partner()
-    for copy in started:
-        copy.wait_send()
-    for spread in spreads:
-        spread.wait_sends()
-
-
-def gather_rows(in_weight, out_weight):
+    pairs = ((send_in, all_in), (send_out, all_out))
+
+    def hop(a, origin, src, sign):
+        return remote(
+            src, pairs[a][1].at[origin, chip, core],
+            zs.at[a, origin, (sign + 1) // 2], zr.at[a, origin], {"shard": shard + sign},
+        )
+
+    def room(sign):
+        return shard + 1 < shards if sign > 0 else shard > 0
+
+    for a, (send, dst) in enumerate(pairs):
+        for sign in (1, -1):
+
+            @pl.when(room(sign))
+            def _():
+                hop(a, shard, send, sign).start()
+
+    for j in range(2 * chips):
+        all_in[shard, j // 2, j % 2] = flat_in[j].astype(half)
+    all_out[shard] = out_ref[...].astype(half)
+    moment = mom_ref[...].T
+    for j in range(2 * chips):
+        mom_rows[j] = moment[j * rows : (j + 1) * rows]
+
+    def far(step, sign):
+        origin = shard - sign * step
+        held = origin >= 0 if sign > 0 else origin < shards
+        return origin, held
+
+    visits = [
+        (a, step, sign)
+        for a in range(2)
+        for step in range(1, shards)
+        for sign in (1, -1)
+    ]
+
+    def spread_of(a, step, sign):
+        origin, held = far(step, sign)
+        dst = pairs[a][1]
+        sems = [ref for ref in (xs, xr, ps, pr)]
+        odd = (step + (sign > 0) + a) % 2 == 1
+        return Spread(lambda block, k: dst.at[origin, block, k], sems, (a, origin), odd), held
+
+    for a, step, sign in visits:
+        origin, held = far(step, sign)
+
+        @pl.when(held)
+        def _():
+            slot = pairs[a][1].at[origin, chip, core]
+            hop(a, origin, slot, sign).wait_recv()
+
+            @pl.when(room(sign))
+            def _():
+                hop(a, origin, slot, sign).start()
+
+            spread_of(a, step, sign)[0].start(0)
+
+    for pattern in range(1, chips):
+        for a, step, sign in visits:
+            spread, held = spread_of(a, step, sign)
+
+            @pl.when(held)
+            def _():
+                spread.wait(pattern)
+                spread.start(pattern)
+
+    for a, step, sign in visits:
+        origin, held = far(step, sign)
+
+        @pl.when(held)
+        def _():
+            spread = spread_of(a, step, sign)[0]
+            spread.wait_partner()
+            spread.wait_sends()
+
+            @pl.when(room(sign))
+            def _():
+                hop(a, origin, pairs[a][1].at[origin, chip, core], sign).wait_send()
+
+    for a, (send, dst) in enumerate(pairs):
+        for sign in (1, -1):
+
+            @pl.when(room(sign))
+            def _():
+                hop(a, shard, send, sign).wait_send()
+
+
+def gather_rows(in_weight, out_weight, in_moment):
     chips = lax.axis_size("rep") // 2
     shards = lax.axis_size("shard")
     half = jnp.bfloat16
-
-    def split(rows):
-        return rows.reshape(chips, 2, rows.shape[0] // (2 * chips), rows.shape[1])
-
-    parts = [split(in_weight), split(out_weight)]
+    f32 = jnp.float32
+    height, columns = in_weight.shape
+    rows = height // (2 * chips)
+    depth = out_weight.shape[1]
+    out_rows = out_weight.shape[0] // (2 * chips)
     vmem = pl.BlockSpec(memory_space=pltpu.VMEM)
     dma = pltpu.SemaphoreType.DMA
-    whole = pl.pallas_call(
+    whole_in, whole_out, moment = pl.pallas_call(
         gather_kernel,
-        out_shape=[jax.ShapeDtypeStruct((shards,) + p.shape, half) for p in parts],
-        in_specs=[vmem, vmem],
-        out_specs=[vmem, vmem],
-        scratch_shapes=[pltpu.VMEM(p.shape[2:], half) for p in parts]
-        + [dma((2, shards))] * 2
+        out_shape=[
+            jax.ShapeDtypeStruct((shards, chips, 2, rows, columns), half),
+            jax.ShapeDtypeStruct((shards, chips, 2, out_rows, depth), half),
+            jax.ShapeDtypeStruct((2 * chips, rows, columns), f32),
+        ],
+        in_specs=[vmem] * 3,
+        out_specs=[vmem] * 3,
+        scratch_shapes=[
+            pltpu.VMEM((2 * chips, rows, columns), f32),
+            pltpu.VMEM((rows, columns), half),
+            pltpu.VMEM((out_rows, depth), half),
+            dma((2, shards, 2)),
+            dma((2, shards)),
+        ]
         + [dma((2, shards, chips))] * 4,
         compiler_params=pltpu.CompilerParams(
             collective_id=0, has_side_effects=True, vmem_limit_bytes=60 * 1024 * 1024
         ),
-    )(*parts)
-    return [
-        w.reshape(shards * p.shape[0], p.shape[1]) for w, p in zip(whole, (in_weight, out_weight))
-    ]
+    )(in_weight.T, out_weight.reshape(chips, 2, out_rows, depth), in_moment.T)
+    return (
+        whole_in.reshape(shards * height, columns),
+        whole_out.reshape(shards * out_weight.shape[0], depth),
+        moment.reshape(chips, 2, rows, columns),
+    )
 
 
 def low_phase(pattern, phases):
     return phases if pattern == 0 else (pattern & -pattern).bit_length() - 1
 
 
-def update_kernel(names, tail, gin, gout, small, inmom, outmom, *refs):
+def update_kernel(names, tail, scale, normed, dproj, mixed, livecot, small, inmom, outmom, *refs):
     k = dict(zip(names, refs))
     rep, shard, core, chip, chips, shards = places()
     f32 = jnp.float32
     half = jnp.bfloat16
     partner = {"rep": 2 * chip + 1 - core}
-    flips = core_flips(chip, core, chips)
-    other_flips = core_flips(chip, 1 - core, chips)
     base_flips = plain_flips(chip, chips)
-    phases = len(flips)
+    phases = len(base_flips)
+    turned = (False, True, True, False)
     wide = k["gl"].shape[-1]
     thin = k["gt"].shape[-1]
     count = 4
@@ -316,7 +383,7 @@
     offsets = (0, wide, 2 * wide)
     widths = (wide, wide, thin)
     owners = [number * shards // count for number in range(count)]
-    order = (0, 1, 3, 2)
+    order = (3, 0, 1, 2)
     line = line_order(shard, shards)
     started = []
 
@@ -325,9 +392,28 @@
         started.append(copy)
 
     def source(number, block, which):
-        if number == 3:
-            return gout.at[:, :, block, which]
-        return gin.at[:, block, which, :, pl.ds(offsets[number], widths[number])]
+        ref = k[f"grad{number}"]
+        return ref.at[:, :, block, which] if number == 3 else ref.at[:, block, which]
+
+    def flips_of(number):
+        return turned_flips(chip, chips, turned[number])
+
+    def own_grad(number):
+        ref = k[f"grad{number}"]
+        first, second = (mixed, livecot) if number == 3 else (normed, dproj)
+        second = second[...]
+        if number < 3:
+            second = second[:, offsets[number] : offsets[number] + (tail if number == 2 else wide)]
+        value = lax.dot_general(
+            first[...], second, (((0,), (0,)), ((), ())), preferred_element_type=f32
+        )
+        value = (scale * value).astype(half)
+        value = value.reshape(ref.shape[:-1] + (value.shape[-1],))
+        if number == 2:
+            ref[...] = jnp.zeros(ref.shape, half)
+            ref[..., :tail] = value
+        else:
+            ref[...] = value
 
     local = [
         pltpu.make_async_copy(inmom.at[chip, core], k["momin"], k["lsem"].at[0]),
@@ -340,15 +426,16 @@
         sorted((d for d in range(1, chips) if low_phase(d, phases) == p), reverse=True)
         for p in range(phases)
     ] + [[0]]
-    patterns = [d for stage in stages for d in stage]
     go(remote(small, k["tcore"], k["ts"].at[0], k["tr"].at[0], partner))
     for stage in ([0], range(1, phases + 1)):
         for number in order:
+            if 0 in stage:
+                own_grad(number)
             for p in stage:
                 for d in stages[p]:
                     go(
                         remote(
-                            source(number, block_at(chip, other_flips, d), 1 - core),
+                            source(number, block_at(chip, flips_of(number), d), 1 - core),
                             k[f"first{number}"].at[d],
                             k["ds"].at[number, d], k["dr"].at[number, d], partner,
                         )
@@ -389,6 +476,7 @@
 
     def reduce_step(number, d):
         last = low_phase(d, phases)
+        flips = flips_of(number)
         slot = k[f"first{number}"].at[d]
         remote(slot, slot, k["ds"].at[number, d], k["dr"].at[number, d], partner).wait_recv()
         total = source(number, block_at(chip, flips, d), core)[...].astype(f32)
@@ -476,11 +564,11 @@
         return lambda block, which: ref.at[number, block, which]
 
     grad_spreads = [
-        Spread(grad_slot(number), [k["g" + s] for s in ("xs", "xr", "ps", "pr")], (number,))
+        Spread(grad_slot(number), [k["g" + s] for s in ("xs", "xr", "ps", "pr")], (number,), turned[number])
         for number in range(count)
     ]
     orth_spreads = [
-        Spread(orth_slot(number), [k["o" + s] for s in ("xs", "xr", "ps", "pr")], (number,))
+        Spread(orth_slot(number), [k["o" + s] for s in ("xs", "xr", "ps", "pr")], (number,), turned[number])
         for number in range(count)
     ]
 
@@ -559,8 +647,11 @@
         gsend = k["gsend" + kind]
         folded = kind == "o"
 
-        def piece(block, which):
-            return buf.at[:, :, block, which] if folded else buf.at[:, block, which]
+        def piece(side):
+            part = buf.at[pl.ds(side * (shards // 2), shards // 2)]
+            if folded:
+                return lambda block, which: part.at[:, :, block, which]
+            return lambda block, which: part.at[:, block, which]
 
         def rows(ref, block, which):
             if kind == "l":
@@ -580,8 +671,12 @@
             buf[:, :, chip, core] = merged
         else:
             buf[:, chip, core] = merged
-        spread = Spread(piece, [k["b" + s] for s in ("xs", "xr", "ps", "pr")], ())
-        spread.start(0)
+        spreads = [
+            Spread(piece(side), [k["b" + s] for s in ("xs", "xr", "ps", "pr")], (side,), side == 1)
+            for side in range(2)
+        ]
+        for spread in spreads:
+            spread.start(0)
         gsend[...] = total.astype(half)
 
         def send_grad(other):
@@ -594,9 +689,11 @@
             send_grad(other).start()
         rows(k["g" + kind], chip, core)[...] = gsend[shard]
         for pattern in range(1, chips):
-            spread.wait(pattern)
-            spread.start(pattern)
-        spread.wait_partner()
+            for spread in spreads:
+                spread.wait(pattern)
+                spread.start(pattern)
+        for spread in spreads:
+            spread.wait_partner()
         matrix = buf[...].reshape(cur.shape).astype(f32)
         frobenius = jnp.sqrt(jnp.sum(matrix * matrix))
         cur[...] = (matrix / (frobenius + 1e-07)).astype(half)
@@ -604,7 +701,8 @@
             iterate_left(cur, k["graml"], k["polyl"])
         else:
             iterate_right(cur, k["gram" + kind], k["poly" + kind])
-        spread.wait_sends()
+        for spread in spreads:
+            spread.wait_sends()
         buf[...] = cur[...].reshape(buf.shape)
 
         def back(other):
@@ -687,22 +785,17 @@
             orth_spreads[number].wait_sends()
 
 
-def reduce_and_orthogonalize(grad_in, grad_out, small, in_moment, out_moment, wide):
+def reduce_and_orthogonalize(normed, dproj, mixed, livecot, scale, small, inmom, out_moment, wide):
     chips = lax.axis_size("rep") // 2
     shards = lax.axis_size("shard")
     half = jnp.bfloat16
     f32 = jnp.float32
-    height, columns = grad_in.shape
-    depth = grad_out.shape[1]
+    height, columns = normed.shape[1], dproj.shape[1]
+    depth = livecot.shape[1]
     rows = height // (shards * chips * 2)
-    folds = grad_out.shape[0] // height
+    folds = mixed.shape[1] // height
     tail = columns - 2 * wide
     thin = -(-tail // LANES) * LANES
-    gin = jnp.pad(grad_in, ((0, 0), (0, thin - tail))).reshape(
-        shards, chips, 2, rows, 2 * wide + thin
-    )
-    gout = grad_out.reshape(shards, folds, chips, 2, rows, depth)
-    inmom = in_moment.reshape(chips, 2, rows, columns)
     outmom = out_moment.reshape(folds, chips, 2, rows, depth)
     outs = {
         "gl": ((2, chips, 2, rows, wide), half),
@@ -724,6 +817,8 @@
         "tz": ((shards,) + small.shape, f32),
     }
     for number, part in enumerate(tails):
+        whole = ((shards, folds) if number == 3 else (shards,)) + (chips, 2, rows, part[-1])
+        scratch[f"grad{number}"] = (whole, half)
         for name in ("first", "sums", "recv"):
             scratch[f"{name}{number}"] = ((chips, shards) + part, half)
     full = {
@@ -757,23 +852,23 @@
     for name in ("ds", "dr", "rs", "rr"):
         sems[name] = (4, chips)
     for name in ("xs", "xr", "ps", "pr"):
-        sems["b" + name] = (chips,)
+        sems["b" + name] = (2, chips)
         sems["g" + name] = (4, chips)
         sems["o" + name] = (4, chips)
     vmem = pl.BlockSpec(memory_space=pltpu.VMEM)
     anywhere = pl.BlockSpec(memory_space=pl.ANY)
     names = list(outs) + list(scratch) + list(sems)
     return pl.pallas_call(
-        functools.partial(update_kernel, names, tail),
+        functools.partial(update_kernel, names, tail, scale),
         out_shape=[jax.ShapeDtypeStruct(s, d) for s, d in outs.values()],
-        in_specs=[vmem] * 3 + [anywhere] * 2,
+        in_specs=[vmem] * 5 + [anywhere] * 2,
         out_specs=[vmem] * len(outs),
         scratch_shapes=[pltpu.VMEM(s, d) for s, d in scratch.values()]
         + [pltpu.SemaphoreType.DMA(s) for s in sems.values()],
         compiler_params=pltpu.CompilerParams(
             collective_id=1, has_side_effects=True, vmem_limit_bytes=60 * 1024 * 1024
         ),
-    )(gin, gout, small, inmom, outmom)
+    )(normed, dproj, mixed, livecot, small, inmom, outmom)
 
 
 def finish_kernel(
@@ -785,17 +880,17 @@
 ):
     f32 = jnp.float32
     wide = gl.shape[-1]
-    tail = in_w.shape[1] - 2 * wide
+    tail = in_w.shape[0] - 2 * wide
     spans = ((0, wide), (wide, wide), (2 * wide, tail))
     for number, (low, width) in enumerate(spans):
         if number < 2:
-            grad, orth = gl[number].astype(f32), ol[number].astype(f32)
+            grad, orth = gl[number].astype(f32).T, ol[number].astype(f32).T
         else:
-            grad, orth = gt[:, :width].astype(f32), ot[:, :width].astype(f32)
+            grad, orth = gt[...].astype(f32).T[:width], ot[...].astype(f32).T[:width]
         here = slice(low, low + width)
-        grad_in[:, here] = grad
-        mom_in[:, here] = momentum_keep * in_m[:, here] + grad
-        new_in[:, here] = muon_apply(in_w[:, here], orth, sizes[number])
+        grad_in[here] = grad
+        mom_in[here] = momentum_keep * in_m[here] + grad
+        new_in[here] = muon_apply(in_w[here], orth, sizes[number])
     grad = go[...].astype(f32)
     grad_out[...] = grad
     mom_out[...] = momentum_keep * out_m[...] + grad
@@ -814,7 +909,7 @@
     taps = p_conv.shape[0]
     conv = tiny[:taps]
     grad_conv[...] = conv
-    n_conv[...], s_conv[0], s_conv[1] = adam(conv, p_conv[...], (a_conv[0], a_conv[1]))
+    n_conv[...], s_conv[:, 0], s_conv[:, 1] = adam(conv, p_conv[...], (a_conv[:, 0], a_conv[:, 1]))
     for row, grad_ref, p, a, n, s in (
         (taps, grad_gate, p_gate, a_gate, n_gate, s_gate),
         (taps + 1, grad_norm, p_norm, a_norm, n_norm, s_norm),
@@ -827,8 +922,8 @@
         grad = tiny[taps + 2 : taps + 3, i * LANES : i * LANES + heads]
         one = slice(i, i + 1)
         grad_head[one] = grad
-        n_head[one], s_head[0, one], s_head[1, one] = adam(
-            grad, p_head[one], (a_head[0, one], a_head[1, one])
+        n_head[one], s_head[i, 0:1], s_head[i, 1:2] = adam(
+            grad, p_head[one], (a_head[i, 0:1], a_head[i, 1:2])
         )
 
 
@@ -865,7 +960,7 @@
 ):
     shards = lax.axis_size("shard")
     replicas = lax.axis_size("rep")
-    whole_in, whole_out = gather_rows(in_weight, out_weight)
+    whole_in, whole_out, moment = gather_rows(in_weight, out_weight, in_moment)
     results = device_pass(
         tokens,
         cotangent,
@@ -880,14 +975,14 @@
         conv_params,
         head_params,
     )
-    activations, input_grad, grad_in, grad_out, grad_norm, grad_gate, grad_conv, grad_head = results
+    activations, input_grad, factors, grad_norm, grad_gate, grad_conv, grad_head = results
     scale = 1.0 / math.sqrt(tokens.shape[0] * shards * replicas)
     wide = gate_gain.shape[0]
     gl, gt, go, ol, ot, oo, tiny = reduce_and_orthogonalize(
-        (scale * grad_in).astype(jnp.bfloat16),
-        (scale * grad_out).astype(jnp.bfloat16),
+        *factors,
+        scale,
         scale * pack_small(grad_norm, grad_gate, grad_conv, grad_head),
-        in_moment,
+        moment,
         out_moment,
         wide,
     )
@@ -903,8 +998,10 @@
     for l, t, o in ((gl, gt, go), (ol, ot, oo)):
         pieces += [l.reshape(2, rows, wide), t.reshape(rows, -1), o.reshape(out_weight.shape)]
     params = [norm_gain[None], gate_gain[None], conv_params, head_params]
-    states = [adam_norm, adam_gate, adam_conv, adam_head]
-    like = [in_weight, out_weight] + params + [in_weight, out_weight] * 2 + params + states
+    states = [adam_norm, adam_gate, jnp.swapaxes(adam_conv, 0, 1), jnp.swapaxes(adam_head, 0, 1)]
+    weights = [in_weight.T, out_weight]
+    moments = [in_moment.T, out_moment]
+    like = weights + params + weights * 2 + params + states
     vmem = pl.BlockSpec(memory_space=pltpu.VMEM)
     done = pl.pallas_call(
         functools.partial(finish_kernel, sizes),
@@ -912,10 +1009,14 @@
         in_specs=[vmem] * (11 + 8),
         out_specs=[vmem] * len(like),
         compiler_params=pltpu.CompilerParams(vmem_limit_bytes=60 * 1024 * 1024),
-    )(*pieces, tiny, in_weight, out_weight, in_moment, out_moment, *params, *states)
+    )(*pieces, tiny, *weights, *moments, *params, *states)
     done = list(done)
     for spot, gain in ((2, norm_gain), (3, gate_gain), (10, norm_gain), (11, gate_gain)):
         done[spot] = done[spot].reshape(gain.shape)
+    for spot in (0, 6, 8):
+        done[spot] = done[spot].T
+    for spot in (16, 17):
+        done[spot] = jnp.swapaxes(done[spot], 0, 1)
     return (activations, input_grad, *done)
 
 

time: 177 us -> 182 us (1.028)
  other arithmetic: 11.1 us -> 21.2 us
  Pallas kernels: 124 us -> 114 us
  matrix products: 19.6 us -> 28.1 us
  local copies, waits for them, and re-layouts: 21.2 us -> 16.3 us
    unnamed x48 -> x98, local copies, waits for them, and re-layouts: 17.2 us -> 5.51 us
    pallas_call x2, Pallas kernels: 119 us -> 109 us  [the longest x1 77 us: reduce_and_orthogonalize(): pl.pallas_call(functools.partial(update_kernel, names, tail, scale), out_...]
    dot_general x3, matrix products: 9.94 us -> 16.1 us  [mixer(): jnp.einsum('hts,shp->thp', decay * scores[None], weighted, precision=ssd_...]
    pad x1 -> x0, local copies, waits for them, and re-layouts: 3.37 us -> none  [reduce_and_orthogonalize(): jnp.pad(grad_in, ((0, 0), (0, thin - tail)))]
    reduce_sum x2, other arithmetic: 1.08 us -> 4.31 us  [mixer(): outputs = outputs + head_params[2][None, :, None] * values]
    reshape x0 -> x2, local copies, waits for them, and re-layouts: none -> 3.11 us  [the longest x1 1.55 us: mixer(): values = activated[:, :width_inner].reshape(total, heads, head_size)]
    dot_general x3, matrix products: 0.81 us -> 3.75 us  [mixer(): scores = jnp.dot(c_input, b_input.T, precision=ssd_precision)]
    dot_general x2 -> x0, matrix products: 2.37 us -> none  [the longest x1 1.5 us: device_pass(): grad_out = jnp.dot(mixed16.T, live_cot, preferred_element_type=jnp.float32)]
where the time goes in v2:
time: 182 us; the launch traced here: 181 us
  Pallas kernels  114 us (63%)
  matrix products  28.1 us (15%)
  other arithmetic  21.2 us (12%)
  local copies, waits for them, and re-layouts  16.3 us (9%)
    pallas_call x1, Pallas kernels, reduce_and_orthogonalize(): pl.pallas_call(functools.partial(update_kernel, names, tail, scale), out_...  77 us
    pallas_call x1, Pallas kernels, gather_rows(): pl.pallas_call(gather_kernel, out_shape=[jax.ShapeDtypeStruct((shards, ch...  31.9 us
    dot_general x3, matrix products, mixer(): jnp.einsum('hts,shp->thp', decay * scores[None], weighted, precision=ssd_...  16.1 us
    unnamed x98, local copies, waits for them, and re-layouts  5.51 us
    pallas_call x1, Pallas kernels, local(): pl.pallas_call(functools.partial(finish_kernel, sizes), out_shape=[jax.Sh...  5.43 us
    reduce_sum x2, other arithmetic, mixer(): outputs = outputs + head_params[2][None, :, None] * values  4.31 us
    dot_general x3, matrix products, mixer(): scores = jnp.dot(c_input, b_input.T, precision=ssd_precision)  3.75 us

profile of v2, /device:TPU:0, one launch (start us, length us, event | category | flops | bytes accessed | tf_op | source)
XLA Modules:
  0.0 181.4 jit_solution(12652409981961807785)
XLA Ops:
  0.7 0.7 fusion.73
  1.4 0.8 reduce-window.9
  2.3 1.1 fusion.43
  3.4 1.3 slice_bitcast_fusion
  4.8 1.1 slice_reduce_fusion.4
  5.9 0.7 fusion.50
  6.6 1.1 fusion.40.normed
  7.7 1.9 %broadcast_select_fusion.livecot = bf16[256,512]{1,0:T(8,128)(2,1)} fusion(bf16[256,512]{1,0:T(8,128)(2,1)} %param.17, pred[256]{0:T(512)(128)(4,1)S(1)} %fusion.73), kind=kLoop, calls=%fused_computation.81 | loop fusion | flops 131072 | bytes 524544 | tf_op jit(solution)/shard_map/jit(_where)/select_n | solution.py:105
  9.6 31.9 %shard_map.311 = (bf16[4,4,2,16,2320]{4,3,2,1,0:T(8,128)(2,1)}, bf16[4,4,2,32,512]{4,3,2,1,0:T(8,128)(2,1)}, f32[8,16,2320]{2,1,0:T(8,128)}) custom-call(f32[2320,128]{1,0:T(8,128)} %bitcast.75, f32[4,2,32,512]{3,2,1,0:T(8,128)} %bitcast.81, f32[2320,128]{1,0:T(8,128)} %bitcast.77), custom_call_target="tpu_custom_call" | custom-call | tf_op jit(solution)/shard_map/pallas_call | solution.py:338
  41.5 2.5 %fusion.84 = f32[256,2320]{1,0:T(8,128)S(1)} fusion(bf16[256,512]{1,0:T(8,128)(2,1)S(1)} %fusion.40.normed, bf16[512,2320]{1,0:T(8,128)(2,1)} %bitcast.79), kind=kOutput, calls=%fused_computation.144 | convolution fusion | flops 608174080 | bytes 5013504 | tf_op jit(solution)/shard_map/dot_general | solution.py:96
  44.2 0.9 fusion.49
  45.0 0.7 copy.93
  46.1 0.8 copy-done.6
  46.9 0.4 copy-done.2
  47.4 2.1 %fusion.29 = (f32[256,1280]{1,0:T(8,128)S(1)}, f32[256,1280]{1,0:T(8,128)}) fusion(f32[256]{0:T(256)S(1)} %get-tuple-element.120, f32[253,1280]{1,0:T(8,128)S(1)} %slice.98, f32[1280]{0:T(1024)S(1)} %get-tuple-element.89, f32[256]{0:T(256)S(1)} %get-tuple-element.121, f32[254,1280]{1,0:T(8,128)S(1)} %slice.97, f32[1280]{0:T(1024)S(1)} %get-tuple-element.86, ...), kind=kLoop, calls=%fused_computation.37 | loop fusion | flops 4915200 | bytes 7862272 | tf_op jit(solution)/shard_map/jvp(jit(silu))/mul | solution.py:52
  49.4 1.1 fusion.59
  50.7 1.3 copy.91
  52.1 5.5 %fusion.24 = f32[256,16,64]{0,2,1:T(8,128)} fusion(f32[256,256]{1,0:T(8,128)} %fusion.59, f32[16,256]{1,0:T(8,128)} %fusion.49, pred[256,256]{1,0:T(8,128)(4,1)} %fusion.50, f32[256,16,64]{0,2,1:T(8,128)} %bitcast.86, f32[16]{0:T(128)} %get-tuple-element.116, f32[256,16]{0,1:T(8,128)} %copy.93), kind=kOutput, calls=%fused_computation.25 | convolution fusion | flops 407633920 | bytes 2457664 | tf_op jit(solution)/shard_map/jvp(hts,shp->thp)/dot_general | solution.py:67
  57.5 1.6 copy.95
  59.1 0.4 multiply_reduce_fusion.9
  59.5 0.5 copy-done.12
  60.0 0.4 copy-done.18
  60.4 1.2 multiply_reduce_fusion.6
  61.7 3.0 %multiply_reduce_fusion.5 = (f32[1024]{0:T(1024)}, f32[256,1024]{1,0:T(8,128)}, f32[256,1024]{1,0:T(8,128)}, bf16[256,1024]{1,0:T(8,128)(2,1)S(1)}) fusion(f32[256,1280]{1,0:T(8,128)S(1)} %copy-done.1, f32[256,2320]{1,0:T(8,128)S(1)} %fusion.84, f32[256,1024]{1,0:T(8,128)S(1)} %get-tuple-element.102, f32[256]{0:T(256)S(1)} %multiply_multiply_fusion.1, ...), kind=kLoop, calls=%fused_computation.44 | loop fusion | flops 5766144 | bytes 7874560 | tf_op jit(solution)/shard_map/transpose(jvp())/reduce_sum | solution.py:70
  64.7 1.1 fusion.31
  65.9 1.4 reduce_sum.197
  67.2 1.3 reduce_sum.198
  68.5 1.3 copy.96
  69.9 6.7 %fusion.7 = (f32[16,256]{1,0:T(8,128)}, f32[16,256]{1,0:T(8,128)}, f32[256,256]{1,0:T(8,128)}) fusion(f32[256,256]{1,0:T(8,128)} %fusion.59, f32[16,256]{1,0:T(8,128)} %fusion.49, pred[256,256]{1,0:T(8,128)(4,1)} %fusion.50, f32[16,64,256]{2,1,0:T(8,128)} %bitcast.88, f32[256,16,64]{0,2,1:T(8,128)} %bitcast.87, f32[256,16]{0,1:T(8,128)} %copy.93), kind=kOutput, calls=%fused_computation.9 | convolution fusion | flops 414375936 | bytes 2752512 | tf_op jit(solution)/shard_map/transpose(jvp(hts,shp->thp))/dot_general | solution.py:67
  76.7 3.9 %multiply_reduce_fusion.7 = (f32[256,16]{0,1:T(8,128)}, f32[256,16,64]{0,2,1:T(8,128)}) fusion(f32[256,1024]{0,1:T(8,128)S(1)} %copy-done.19, f32[256,16]{0,1:T(8,128)S(1)} %copy-done.32, f32[256,16,64]{0,2,1:T(8,128)S(1)} %bitcast.89, f32[16]{0:T(128)S(1)} %copy-done.48, f32[16,64,256]{2,1,0:T(8,128)S(1)} %bitcast.90, f32[256,256]{1,0:T(8,128)S(1)} %copy-done.22, ...), kind=kOutput, calls=%fused_computation.47 | convolution fusion | flops 408154112 | bytes 4571200 | tf_op jit(solution)/shard_map/transpose(jvp(hts,shp->thp))/dot_general | solution.py:67
  80.6 1.6 copy.101
  82.2 1.5 copy.98
  83.6 1.4 fusion.80
  85.1 0.7 bitcast_multiply_fusion
  85.8 0.7 pad_add_fusion.1
  86.4 1.4 fusion.61
  87.8 1.3 fusion.57
  89.1 2.1 %multiply_reduce_fusion.4 = (f32[1280]{0:T(1024)S(1)}, f32[256,1280]{1,0:T(8,128)S(1)}, f32[256,1280]{1,0:T(8,128)S(1)}) fusion(f32[253,1280]{1,0:T(8,128)S(1)} %copy-done.7, f32[256]{0:T(256)S(1)} %copy-done.42, f32[256,1280]{1,0:T(8,128)} %get-tuple-element.104, f32[256,1024]{1,0:T(8,128)S(1)} %copy.101, f32[256,128]{1,0:T(8,128)S(1)} %fusion.61, ...), kind=kLoop, calls=%fused_computation.34 | loop fusion | flops 4586240 | bytes 6544384 | tf_op jit(solution)/shard_map/transpose(jvp())/reduce_sum | solution.py:51
  91.4 0.5 multiply_reduce_fusion.3
  92.2 0.6 copy-done.24
  93.0 0.4 multiply_reduce_fusion.1
  93.5 0.8 copy-done.9
  94.4 1.6 copy-done.11
  96.0 1.0 fusion.41
  97.0 0.6 fusion.66.small
  97.6 77.0 %shard_map.312 = (bf16[2,4,2,16,1024]{4,3,2,1,0:T(8,128)(2,1)}, bf16[4,2,16,384]{3,2,1,0:T(8,128)(2,1)}, bf16[2,4,2,16,512]{4,3,2,1,0:T(8,128)(2,1)}, bf16[2,4,2...) custom-call(bf16[256,512]{1,0:T(8,128)(2,1)} %copy-done.13, ...), custom_call_target="tpu_custom_call" | custom-call | tf_op jit(solution)/shard_map/pallas_call | solution.py:861
  174.7 1.0 fusion.42
  175.8 5.4 %shard_map.313 = (f32[2320,128]{1,0:T(8,128)}, f32[256,512]{1,0:T(8,128)}, f32[1,512]{1,0:T(1,128)}, f32[1,1024]{1,0:T(1,128)}, f32[5,1280]{1,0:T(8,128)}, /*ind...) custom-call(bf16[2,128,1024]{2,1,0:T(8,128)(2,1)} %bitcast.93, ...), custom_call_target="tpu_custom_call" | custom-call | tf_op jit(solution)/shard_map/pallas_call | solution.py:1006
  (114 shorter events, 1.7 us)
Async XLA Ops:
  1.4 40.1 %copy-start.43 = (pred[256]{0:T(512)(128)(4,1)}, pred[256]{0:T(512)(128)(4,1)S(1)}, u32[]{:S(2)}) copy-start(pred[256]{0:T(512)(128)(4,1)S(1)} %fusion.73) | copy-start | bytes 772
  3.4 38.1 %copy-start.33 = (f32[256]{0:T(256)}, f32[256]{0:T(256)S(1)}, u32[]{:S(2)}) copy-start(f32[256]{0:T(256)S(1)} %fusion.43) | copy-start | bytes 3076
  3.4 38.1 %copy-start.35 = (f32[256]{0:T(256)}, f32[256]{0:T(256)S(1)}, u32[]{:S(2)}) copy-start(f32[256]{0:T(256)S(1)} %fusion.74) | copy-start | bytes 3076
  4.7 39.4 %copy-start.47 = (f32[16]{0:T(128)}, f32[16]{0:T(128)S(1)}, u32[]{:S(2)}) copy-start(f32[16]{0:T(128)S(1)} %get-tuple-element.118) | copy-start | bytes 196
  4.7 39.5 %copy-start.46 = (f32[16]{0:T(128)}, f32[16]{0:T(128)S(1)}, u32[]{:S(2)}) copy-start(f32[16]{0:T(128)S(1)} %get-tuple-element.117) | copy-start | bytes 196
  4.8 41.2 %copy-start.37 = (f32[256]{0:T(256)}, f32[256]{0:T(256)S(1)}, u32[]{:S(2)}) copy-start(f32[256]{0:T(256)S(1)} %get-tuple-element.119) | copy-start | bytes 3076
  4.8 41.3 %copy-start.39 = (f32[256]{0:T(256)}, f32[256]{0:T(256)S(1)}, u32[]{:S(2)}) copy-start(f32[256]{0:T(256)S(1)} %get-tuple-element.121) | copy-start | bytes 3076
  4.8 41.3 %copy-start.41 = (f32[256]{0:T(256)}, f32[256]{0:T(256)S(1)}, u32[]{:S(2)}) copy-start(f32[256]{0:T(256)S(1)} %get-tuple-element.120) | copy-start | bytes 3076
  5.9 40.2 %copy-start.23 = (f32[1280]{0:T(1024)}, f32[1280]{0:T(1024)S(1)}, u32[]{:S(2)}) copy-start(f32[1280]{0:T(1024)S(1)} %get-tuple-element.87) | copy-start | bytes 15364
  5.9 40.2 %copy-start.25 = (f32[1280]{0:T(1024)}, f32[1280]{0:T(1024)S(1)}, u32[]{:S(2)}) copy-start(f32[1280]{0:T(1024)S(1)} %get-tuple-element.86) | copy-start | bytes 15364
  7.7 33.8 %copy-start.13 = (bf16[256,512]{1,0:T(8,128)(2,1)}, bf16[256,512]{1,0:T(8,128)(2,1)S(1)}, u32[]{:S(2)}) copy-start(bf16[256,512]{1,0:T(8,128)(2,1)S(1)} %fusion.40.normed) | copy-start | bytes 786436
  44.2 1.6 copy-start.17
  45.8 1.1 copy-start.6
  45.9 1.4 copy-start.2
  47.4 2.1 %copy-start.4 = (f32[255,1280]{1,0:T(8,128)}, f32[255,1280]{1,0:T(8,128)S(1)}, u32[]{:S(2)}) copy-start(f32[255,1280]{1,0:T(8,128)S(1)} %slice.96) | copy-start | bytes 3916804
  49.4 1.2 copy-start
  59.1 1.0 copy-start.12
  59.1 1.3 copy-start.18
  59.1 1.3 copy-start.28
  60.4 1.3 copy-start.1
  61.7 3.0 %copy-start.14 = (bf16[256,512]{1,0:T(8,128)(2,1)S(1)}, bf16[256,512]{1,0:T(8,128)(2,1)}, u32[]{:S(2)}) copy-start(bf16[256,512]{1,0:T(8,128)(2,1)} %param.16) | copy-start | bytes 786436
  61.7 3.0 %copy-start.44 = (pred[256]{0:T(512)(128)(4,1)S(1)}, pred[256]{0:T(512)(128)(4,1)}, u32[]{:S(2)}) copy-start(pred[256]{0:T(512)(128)(4,1)} %copy-done.43) | copy-start | bytes 772
  64.7 1.2 copy-start.16
  64.7 3.8 %copy-start.10 = (f32[256,1024]{1,0:T(8,128)S(1)}, f32[256,1024]{1,0:T(8,128)}, u32[]{:S(2)}) copy-start(f32[256,1024]{1,0:T(8,128)} %get-tuple-element.98) | copy-start | bytes 3145732
  69.8 6.8 %copy-start.19 = (f32[256,1024]{0,1:T(8,128)S(1)}, f32[256,1024]{0,1:T(8,128)}, u32[]{:S(2)}) copy-start(f32[256,1024]{0,1:T(8,128)} %copy.91) | copy-start | bytes 3145732
  69.8 6.8 %copy-start.20 = (f32[256,1024]{0,1:T(8,128)S(1)}, f32[256,1024]{0,1:T(8,128)}, u32[]{:S(2)}) copy-start(f32[256,1024]{0,1:T(8,128)} %copy.96) | copy-start | bytes 3145732
  69.8 6.8 %copy-start.22 = (f32[256,256]{1,0:T(8,128)S(1)}, f32[256,256]{1,0:T(8,128)}, u32[]{:S(2)}) copy-start(f32[256,256]{1,0:T(8,128)} %fusion.59) | copy-start | bytes 786436
  69.9 6.8 %copy-start.27 = (pred[256,256]{1,0:T(8,128)(4,1)S(1)}, pred[256,256]{1,0:T(8,128)(4,1)}, u32[]{:S(2)}) copy-start(pred[256,256]{1,0:T(8,128)(4,1)} %fusion.50) | copy-start | bytes 196612
  69.9 6.8 %copy-start.31 = (f32[16,256]{1,0:T(8,128)S(1)}, f32[16,256]{1,0:T(8,128)}, u32[]{:S(2)}) copy-start(f32[16,256]{1,0:T(8,128)} %fusion.49) | copy-start | bytes 49156
  69.9 6.8 %copy-start.32 = (f32[256,16]{0,1:T(8,128)S(1)}, f32[256,16]{0,1:T(8,128)}, u32[]{:S(2)}) copy-start(f32[256,16]{0,1:T(8,128)} %copy.93) | copy-start | bytes 49156
  69.9 6.8 %copy-start.48 = (f32[16]{0:T(128)S(1)}, f32[16]{0:T(128)}, u32[]{:S(2)}) copy-start(f32[16]{0:T(128)} %get-tuple-element.116) | copy-start | bytes 196
  83.6 5.5 %copy-start.7 = (f32[253,1280]{1,0:T(8,128)S(1)}, f32[253,1280]{1,0:T(8,128)}, u32[]{:S(2)}) copy-start(f32[253,1280]{1,0:T(8,128)} %copy-done.6) | copy-start | bytes 3886084
  83.6 5.5 %copy-start.42 = (f32[256]{0:T(256)S(1)}, f32[256]{0:T(256)}, u32[]{:S(2)}) copy-start(f32[256]{0:T(256)} %copy-done.41) | copy-start | bytes 3076
  89.1 2.2 %copy-start.3 = (f32[254,1280]{1,0:T(8,128)S(1)}, f32[254,1280]{1,0:T(8,128)}, u32[]{:S(2)}) copy-start(f32[254,1280]{1,0:T(8,128)} %copy-done.2) | copy-start | bytes 3901444
  89.1 2.2 %copy-start.5 = (f32[255,1280]{1,0:T(8,128)S(1)}, f32[255,1280]{1,0:T(8,128)}, u32[]{:S(2)}) copy-start(f32[255,1280]{1,0:T(8,128)} %copy-done.4) | copy-start | bytes 3916804
  89.1 2.2 %copy-start.38 = (f32[256]{0:T(256)S(1)}, f32[256]{0:T(256)}, u32[]{:S(2)}) copy-start(f32[256]{0:T(256)} %copy-done.37) | copy-start | bytes 3076
  89.1 2.2 %copy-start.40 = (f32[256]{0:T(256)S(1)}, f32[256]{0:T(256)}, u32[]{:S(2)}) copy-start(f32[256]{0:T(256)} %copy-done.39) | copy-start | bytes 3076
  91.3 0.7 copy-start.26
  93.0 1.2 copy-start.9
  94.2 1.7 copy-start.11
  94.2 1.7 copy-start.15
  94.3 1.7 copy-start.29
  94.3 1.7 copy-start.36
  96.0 1.0 copy-start.8
  96.0 1.0 copy-start.30
  97.6 77.1 %copy-start.34 = (f32[256]{0:T(256)S(1)}, f32[256]{0:T(256)}, u32[]{:S(2)}) copy-start(f32[256]{0:T(256)} %copy-done.33) | copy-start | bytes 3076
  97.6 77.1 %copy-start.21 = (bf16[256,512]{1,0:T(8,128)(2,1)S(1)}, bf16[256,512]{1,0:T(8,128)(2,1)}, u32[]{:S(2)}) copy-start(bf16[256,512]{1,0:T(8,128)(2,1)} %param.17) | copy-start | bytes 786436
  97.6 77.1 %copy-start.45 = (pred[256]{0:T(512)(128)(4,1)S(1)}, pred[256]{0:T(512)(128)(4,1)}, u32[]{:S(2)}) copy-start(pred[256]{0:T(512)(128)(4,1)} %copy-done.43) | copy-start | bytes 772
  (1 other events, 0.7 us)

commit v3 on v2

--- a/solution.py
+++ b/solution.py
@@ -109,7 +109,7 @@
     d_normed = jnp.dot(d_proj16, back_in.T, preferred_element_type=jnp.float32)
     d_base, grad_norm = norm_back(d_normed)
     input_grad = live_cot.astype(jnp.float32) + d_base
-    factors = (normed16, d_proj16, mixed16, live_cot)
+    factors = (normed16, d_proj16.T, mixed16.T, live_cot)
     return (activations, input_grad, factors, grad_norm, grad_gate, grad_conv, grad_head)
 
 
@@ -400,13 +400,14 @@
 
     def own_grad(number):
         ref = k[f"grad{number}"]
-        first, second = (mixed, livecot) if number == 3 else (normed, dproj)
-        second = second[...]
-        if number < 3:
-            second = second[:, offsets[number] : offsets[number] + (tail if number == 2 else wide)]
-        value = lax.dot_general(
-            first[...], second, (((0,), (0,)), ((), ())), preferred_element_type=f32
-        )
+        if number == 3:
+            value = jnp.dot(mixed[...], livecot[...], preferred_element_type=f32)
+        else:
+            low = offsets[number]
+            part = dproj[low : low + (tail if number == 2 else wide)]
+            value = lax.dot_general(
+                normed[...].T, part, (((1,), (1,)), ((), ())), preferred_element_type=f32
+            )
         value = (scale * value).astype(half)
         value = value.reshape(ref.shape[:-1] + (value.shape[-1],))
         if number == 2:
@@ -790,10 +791,10 @@
     shards = lax.axis_size("shard")
     half = jnp.bfloat16
     f32 = jnp.float32
-    height, columns = normed.shape[1], dproj.shape[1]
+    height, columns = normed.shape[1], dproj.shape[0]
     depth = livecot.shape[1]
     rows = height // (shards * chips * 2)
-    folds = mixed.shape[1] // height
+    folds = mixed.shape[0] // height
     tail = columns - 2 * wide
     thin = -(-tail // LANES) * LANES
     outmom = out_moment.reshape(folds, chips, 2, rows, depth)

time: 182 us -> 162 us (0.89)
  local copies, waits for them, and re-layouts: 16.3 us -> 5.02 us
  matrix products: 28.1 us -> 21.2 us
  other arithmetic: 21.2 us -> 18.9 us
    dot_general x3, matrix products: 16.1 us -> 12.1 us  [mixer(): jnp.einsum('hts,shp->thp', decay * scores[None], weighted, precision=ssd_...]
    reshape x2 -> x0, local copies, waits for them, and re-layouts: 3.11 us -> none  [the longest x1 1.55 us: mixer(): values = activated[:, :width_inner].reshape(total, heads, head_size)]
    reduce_sum x2, other arithmetic: 4.31 us -> 1.44 us  [mixer(): outputs = outputs + head_params[2][None, :, None] * values]
    unnamed x98 -> x80, local copies, waits for them, and re-layouts: 5.51 us -> 3.38 us
where the time goes in v3:
time: 162 us; the launch traced here: 161 us
  Pallas kernels  114 us (70%)
  matrix products  21.2 us (13%)
  other arithmetic  18.9 us (12%)
  local copies, waits for them, and re-layouts  5.02 us (3%)
    pallas_call x1, Pallas kernels, reduce_and_orthogonalize(): pl.pallas_call(functools.partial(update_kernel, names, tail, scale), out_...  76.9 us
    pallas_call x1, Pallas kernels, gather_rows(): pl.pallas_call(gather_kernel, out_shape=[jax.ShapeDtypeStruct((shards, ch...  32 us
    dot_general x3, matrix products, mixer(): jnp.einsum('hts,shp->thp', decay * scores[None], weighted, precision=ssd_...  12.1 us
    pallas_call x1, Pallas kernels, local(): pl.pallas_call(functools.partial(finish_kernel, sizes), out_shape=[jax.Sh...  5.53 us
    unnamed x80, local copies, waits for them, and re-layouts  3.38 us

profile of v3, /device:TPU:0, one launch (start us, length us, event | category | flops | bytes accessed | tf_op | source)
XLA Modules:
  0.0 161.0 jit_solution(10408362622714144251)
XLA Ops:
  0.7 0.7 fusion.70
  1.4 0.8 reduce-window.9
  2.3 1.1 fusion.43
  3.4 0.8 slice_bitcast_fusion
  4.2 0.1 compare_convert_fusion.2
  4.3 1.1 slice_reduce_fusion.4
  5.4 0.1 fusion.50
  5.5 1.1 fusion.40.normed
  6.6 1.1 broadcast_select_fusion.livecot
  7.8 32.0 %shard_map.311 = (bf16[4,4,2,16,2320]{4,3,2,1,0:T(8,128)(2,1)}, bf16[4,4,2,32,512]{4,3,2,1,0:T(8,128)(2,1)}, f32[8,16,2320]{2,1,0:T(8,128)}) custom-call(f32[2320,128]{1,0:T(8,128)} %bitcast.82, f32[4,2,32,512]{3,2,1,0:T(8,128)} %bitcast.88, f32[2320,128]{1,0:T(8,128)} %bitcast.84), custom_call_target="tpu_custom_call" | custom-call | tf_op jit(solution)/shard_map/pallas_call | solution.py:338
  39.8 2.8 %fusion.83 = f32[256,2320]{0,1:T(8,128)S(1)} fusion(bf16[256,512]{1,0:T(8,128)(2,1)S(1)} %fusion.40.normed, bf16[512,2320]{1,0:T(8,128)(2,1)} %bitcast.86), kind=kOutput, calls=%fused_computation.147 | convolution fusion | flops 608174080 | bytes 5013504 | tf_op jit(solution)/shard_map/dot_general | solution.py:96
  42.6 0.1 compare_select_fusion.2
  42.7 0.2 fusion.49
  42.9 0.1 slice.98
  43.0 0.1 slice.97
  43.2 0.1 slice.96
  43.3 0.9 copy-done.5
  44.1 0.4 copy-done.1
  44.6 3.0 %fusion.29 = (f32[256,1280]{0,1:T(8,128)S(1)}, f32[256,1280]{0,1:T(8,128)}) fusion(f32[256]{0:T(256)S(1)} %get-tuple-element.120, f32[253,1280]{0,1:T(8,128)S(1)} %slice.98, f32[1280]{0:T(1024)S(1)} %get-tuple-element.89, f32[256]{0:T(256)S(1)} %get-tuple-element.121, f32[254,1280]{0,1:T(8,128)S(1)} %slice.97, f32[1280]{0:T(1024)S(1)} %get-tuple-element.86, ...), kind=kLoop, calls=%fused_computation.37 | loop fusion | flops 4915200 | bytes 7862272 | tf_op jit(solution)/shard_map/jvp(jit(silu))/mul | solution.py:52
  47.6 0.3 fusion.53
  48.0 2.7 %fusion.24 = f32[256,16,64]{0,2,1:T(8,128)S(1)} fusion(f32[256,256]{1,0:T(8,128)S(1)} %fusion.53, f32[16,256]{1,0:T(8,128)S(1)} %fusion.49, pred[256,256]{1,0:T(8,128)(4,1)S(1)} %fusion.50, f32[256,16,64]{0,2,1:T(8,128)S(1)} %bitcast.96, f32[16]{0:T(128)S(1)} %get-tuple-element.116, f32[256,16]{0,1:T(8,128)S(1)} %compare_select_fusion.2), kind=kOutput, calls=%fused_computation.25 | convolution fusion | flops 407633920 | bytes 2457664 | tf_op jit(solution)/shard_map/jvp(hts,shp->thp)/dot_general | solution.py:67
  50.7 0.4 multiply_reduce_fusion.9
  51.1 0.5 copy-done.11
  51.7 0.4 copy-done.13
  52.0 1.5 fusion.31
  53.5 0.6 multiply_reduce_fusion.6
  54.1 1.3 multiply_reduce_fusion.5
  55.4 5.1 %fusion.7 = (f32[16,256]{1,0:T(8,128)}, f32[16,256]{1,0:T(8,128)}, f32[256,256]{1,0:T(8,128)}) fusion(f32[256,256]{1,0:T(8,128)S(1)} %fusion.53, f32[16,256]{1,0:T(8,128)S(1)} %fusion.49, pred[256,256]{1,0:T(8,128)(4,1)S(1)} %fusion.50, f32[16,64,256]{2,1,0:T(8,128)S(1)} %bitcast.93, f32[256,16,64]{0,2,1:T(8,128)S(1)} %bitcast.97, ...), kind=kOutput, calls=%fused_computation.8 | convolution fusion | flops 414375936 | bytes 2752512 | tf_op jit(solution)/shard_map/transpose(jvp(hts,shp->thp))/dot_general | solution.py:67
  60.6 0.1 reduce_sum.198
  60.7 1.2 fusion.55
  62.0 4.4 %multiply_reduce_fusion.7 = (f32[256,16]{0,1:T(8,128)S(1)}, f32[256,16,64]{0,2,1:T(8,128)S(1)}) fusion(f32[256,1280]{0,1:T(8,128)} %copy-done, f32[256,16]{0,1:T(8,128)S(1)} %compare_select_fusion.2, f32[256,16,64]{0,2,1:T(8,128)} %bitcast.94, f32[16]{0:T(128)} %copy-done.36, f32[16,64,256]{2,1,0:T(8,128)} %bitcast.95, f32[256,256]{1,0:T(8,128)} %copy-done.17, ...), kind=kOutput, calls=%fused_computation.49 | convolution fusion | flops 408154112 | bytes 4588032 | tf_op jit(solution)/shard_map/transpose(jvp(hts,shp->thp))/dot_general | solution.py:67
  66.4 1.2 fusion.51
  67.6 0.3 fusion.80
  68.0 0.8 multiply_reduce_fusion.4
  68.8 0.7 bitcast_multiply_fusion.2
  69.6 0.1 copy-done.4
  69.7 1.3 multiply_reduce_fusion.3
  71.0 0.6 slice_multiply_fusion.1
  71.6 0.6 slice_multiply_fusion
  72.2 0.6 slice_multiply_fusion.2
  72.8 0.7 multiply_reduce_fusion.1
  73.5 0.9 copy-done.8
  74.5 1.0 fusion.41
  75.6 1.0 fusion.42
  76.6 0.6 fusion.58.small
  77.3 1.1 fusion.75.dproj
  78.4 76.9 %shard_map.312 = (bf16[2,4,2,16,1024]{4,3,2,1,0:T(8,128)(2,1)}, bf16[4,2,16,384]{3,2,1,0:T(8,128)(2,1)}, bf16[2,4,2,16,512]{4,3,2,1,0:T(8,128)(2,1)}, bf16[2,4,2...) custom-call(bf16[256,512]{1,0:T(8,128)(2,1)} %copy-done.10, ...), custom_call_target="tpu_custom_call" | custom-call | tf_op jit(solution)/shard_map/pallas_call | solution.py:862
  155.3 5.5 %shard_map.313 = (f32[2320,128]{1,0:T(8,128)}, f32[256,512]{1,0:T(8,128)}, f32[1,512]{1,0:T(1,128)}, f32[1,1024]{1,0:T(1,128)}, f32[5,1280]{1,0:T(8,128)}, /*ind...) custom-call(bf16[2,128,1024]{2,1,0:T(8,128)(2,1)} %bitcast.99, ...), custom_call_target="tpu_custom_call" | custom-call | tf_op jit(solution)/shard_map/pallas_call | solution.py:1007
  (90 shorter events, 0.5 us)
Async XLA Ops:
  1.4 49.7 %copy-start.30 = (pred[256]{0:T(512)(128)(4,1)}, pred[256]{0:T(512)(128)(4,1)S(1)}, u32[]{:S(2)}) copy-start(pred[256]{0:T(512)(128)(4,1)S(1)} %fusion.70) | copy-start | bytes 772
  3.4 36.4 %copy-start.20 = (f32[256]{0:T(256)}, f32[256]{0:T(256)S(1)}, u32[]{:S(2)}) copy-start(f32[256]{0:T(256)S(1)} %fusion.43) | copy-start | bytes 3076
  3.4 36.4 %copy-start.22 = (f32[256]{0:T(256)}, f32[256]{0:T(256)S(1)}, u32[]{:S(2)}) copy-start(f32[256]{0:T(256)S(1)} %fusion.71) | copy-start | bytes 3076
  4.2 38.4 %copy-start.32 = (f32[16]{0:T(128)}, f32[16]{0:T(128)S(1)}, u32[]{:S(2)}) copy-start(f32[16]{0:T(128)S(1)} %get-tuple-element.118) | copy-start | bytes 196
  4.2 38.5 %copy-start.34 = (f32[16]{0:T(128)}, f32[16]{0:T(128)S(1)}, u32[]{:S(2)}) copy-start(f32[16]{0:T(128)S(1)} %get-tuple-element.117) | copy-start | bytes 196
  4.2 43.8 %copy-start.36 = (f32[16]{0:T(128)}, f32[16]{0:T(128)S(1)}, u32[]{:S(2)}) copy-start(f32[16]{0:T(128)S(1)} %get-tuple-element.116) | copy-start | bytes 196
  4.3 38.9 %copy-start.24 = (f32[256]{0:T(256)}, f32[256]{0:T(256)S(1)}, u32[]{:S(2)}) copy-start(f32[256]{0:T(256)S(1)} %get-tuple-element.119) | copy-start | bytes 3076
  4.3 39.0 %copy-start.26 = (f32[256]{0:T(256)}, f32[256]{0:T(256)S(1)}, u32[]{:S(2)}) copy-start(f32[256]{0:T(256)S(1)} %get-tuple-element.121) | copy-start | bytes 3076
  4.3 39.0 %copy-start.28 = (f32[256]{0:T(256)}, f32[256]{0:T(256)S(1)}, u32[]{:S(2)}) copy-start(f32[256]{0:T(256)S(1)} %get-tuple-element.120) | copy-start | bytes 3076
  6.6 33.2 %copy-start.10 = (bf16[256,512]{1,0:T(8,128)(2,1)}, bf16[256,512]{1,0:T(8,128)(2,1)S(1)}, u32[]{:S(2)}) copy-start(bf16[256,512]{1,0:T(8,128)(2,1)S(1)} %fusion.40.normed) | copy-start | bytes 786436
  7.8 45.8 %copy-start.9 = (bf16[256,512]{1,0:T(8,128)(2,1)}, bf16[256,512]{1,0:T(8,128)(2,1)S(1)}, u32[]{:S(2)}) copy-start(bf16[256,512]{1,0:T(8,128)(2,1)S(1)} %broadcast_select_fusion.livecot) | copy-start | bytes 786436
  42.9 12.6 %copy-start.37 = (f32[16,256]{1,0:T(8,128)}, f32[16,256]{1,0:T(8,128)S(1)}, u32[]{:S(2)}) copy-start(f32[16,256]{1,0:T(8,128)S(1)} %fusion.49) | copy-start | bytes 49156
  43.0 1.1 copy-start.5
  43.1 1.4 copy-start.1
  44.6 3.0 %copy-start.3 = (f32[255,1280]{0,1:T(8,128)}, f32[255,1280]{0,1:T(8,128)S(1)}, u32[]{:S(2)}) copy-start(f32[255,1280]{0,1:T(8,128)S(1)} %slice.96) | copy-start | bytes 3916804
  47.6 6.5 %copy-start = (f32[256,1280]{0,1:T(8,128)}, f32[256,1280]{0,1:T(8,128)S(1)}, u32[]{:S(2)}) copy-start(f32[256,1280]{0,1:T(8,128)S(1)} %get-tuple-element.103) | copy-start | bytes 3932164
  47.9 7.5 %copy-start.17 = (f32[256,256]{1,0:T(8,128)}, f32[256,256]{1,0:T(8,128)S(1)}, u32[]{:S(2)}) copy-start(f32[256,256]{1,0:T(8,128)S(1)} %fusion.53) | copy-start | bytes 786436
  50.7 1.0 copy-start.11
  50.7 1.3 copy-start.13
  50.7 1.3 copy-start.18
  55.4 5.1 %copy-start.14 = (f32[256,1024]{0,1:T(8,128)}, f32[256,1024]{0,1:T(8,128)S(1)}, u32[]{:S(2)}) copy-start(f32[256,1024]{0,1:T(8,128)S(1)} %get-tuple-element.98) | copy-start | bytes 3145732
  61.9 4.5 %copy-start.15 = (f32[256,256]{1,0:T(8,128)S(1)}, f32[256,256]{1,0:T(8,128)}, u32[]{:S(2)}) copy-start(f32[256,256]{1,0:T(8,128)} %get-tuple-element.78) | copy-start | bytes 786436
  61.9 5.7 %copy-start.33 = (f32[16]{0:T(128)S(1)}, f32[16]{0:T(128)}, u32[]{:S(2)}) copy-start(f32[16]{0:T(128)} %copy-done.32) | copy-start | bytes 196
  61.9 5.7 %copy-start.35 = (f32[16]{0:T(128)S(1)}, f32[16]{0:T(128)}, u32[]{:S(2)}) copy-start(f32[16]{0:T(128)} %copy-done.34) | copy-start | bytes 196
  61.9 5.7 %copy-start.38 = (f32[16,256]{1,0:T(8,128)S(1)}, f32[16,256]{1,0:T(8,128)}, u32[]{:S(2)}) copy-start(f32[16,256]{1,0:T(8,128)} %get-tuple-element.76) | copy-start | bytes 49156
  62.0 5.7 %copy-start.39 = (f32[16,256]{1,0:T(8,128)S(1)}, f32[16,256]{1,0:T(8,128)}, u32[]{:S(2)}) copy-start(f32[16,256]{1,0:T(8,128)} %get-tuple-element.77) | copy-start | bytes 49156
  62.0 6.0 %copy-start.6 = (f32[253,1280]{0,1:T(8,128)S(1)}, f32[253,1280]{0,1:T(8,128)}, u32[]{:S(2)}) copy-start(f32[253,1280]{0,1:T(8,128)} %copy-done.5) | copy-start | bytes 3886084
  62.0 6.0 %copy-start.7 = (f32[256,1280]{0,1:T(8,128)S(1)}, f32[256,1280]{0,1:T(8,128)}, u32[]{:S(2)}) copy-start(f32[256,1280]{0,1:T(8,128)} %get-tuple-element.104) | copy-start | bytes 3932164
  62.0 6.0 %copy-start.29 = (f32[256]{0:T(256)S(1)}, f32[256]{0:T(256)}, u32[]{:S(2)}) copy-start(f32[256]{0:T(256)} %copy-done.28) | copy-start | bytes 3076
  68.0 1.6 %copy-start.2 = (f32[254,1280]{0,1:T(8,128)S(1)}, f32[254,1280]{0,1:T(8,128)}, u32[]{:S(2)}) copy-start(f32[254,1280]{0,1:T(8,128)} %copy-done.1) | copy-start | bytes 3901444
  68.0 1.7 %copy-start.4 = (f32[255,1280]{0,1:T(8,128)S(1)}, f32[255,1280]{0,1:T(8,128)}, u32[]{:S(2)}) copy-start(f32[255,1280]{0,1:T(8,128)} %copy-done.3) | copy-start | bytes 3916804
  68.0 1.7 %copy-start.25 = (f32[256]{0:T(256)S(1)}, f32[256]{0:T(256)}, u32[]{:S(2)}) copy-start(f32[256]{0:T(256)} %copy-done.24) | copy-start | bytes 3076
  68.0 1.7 %copy-start.27 = (f32[256]{0:T(256)S(1)}, f32[256]{0:T(256)}, u32[]{:S(2)}) copy-start(f32[256]{0:T(256)} %copy-done.26) | copy-start | bytes 3076
  72.7 1.7 %copy-start.8 = (bf16[4,4,2,16,2320]{4,3,2,1,0:T(8,128)(2,1)S(1)}, bf16[4,4,2,16,2320]{4,3,2,1,0:T(8,128)(2,1)}, u32[]{:S(2)}) copy-start(bf16[4,4,2,16,2320]{4,3,2,1,0:T(8,128)(2,1)} %get-tuple-element.48) | copy-start | bytes 7127044
  72.8 1.7 %copy-start.12 = (bf16[256,512]{1,0:T(8,128)(2,1)S(1)}, bf16[256,512]{1,0:T(8,128)(2,1)}, u32[]{:S(2)}) copy-start(bf16[256,512]{1,0:T(8,128)(2,1)} %param.16) | copy-start | bytes 786436
  72.8 1.7 %copy-start.19 = (f32[512]{0:T(512)S(1)}, f32[512]{0:T(512)}, u32[]{:S(2)}) copy-start(f32[512]{0:T(512)} %param.24) | copy-start | bytes 6148
  72.8 1.7 %copy-start.23 = (f32[256]{0:T(256)S(1)}, f32[256]{0:T(256)}, u32[]{:S(2)}) copy-start(f32[256]{0:T(256)} %copy-done.22) | copy-start | bytes 3076
  74.5 1.1 copy-start.21
  74.5 1.1 copy-start.16
  74.5 1.1 copy-start.31
